TPU v7x, 32 devices: a whole 2x2x4 slice. The times are simulated.
32 devices in a mesh: groups: 2 (over x), seq: 8 (over z, y), chan: 2 (over core).
Axes of the slice: x: 2, y: 2, z: 4, core: 2. Of those that a mesh axis runs over, the one named last changes fastest.
Arguments:
- inputs: bfloat16 [8192, 768], P(('groups', 'seq')), parts along dimension 0, may hold values from -6 to 6
- enc_weight: bfloat16 [768, 5, 1536], P('seq', None, 'chan'), may hold values from -0.09375 to 0.09375
- dec_weight: bfloat16 [768, 5, 1536], P('seq', None, 'chan'), may hold values from -0.0625 to 0.0625
- cotangent: bfloat16 [8192, 768], P(('groups', 'seq'), 'chan'), parts along dimension 0, may hold values from -6 to 6
Outputs:
- mixed_out: bfloat16 [8192, 768], P(('groups', 'seq'), 'chan'), parts along dimension 0
- input_grad: bfloat16 [8192, 768], P(('groups', 'seq'), 'chan'), parts along dimension 0
- enc_grad: bfloat16 [1536, 5, 1536], P(('groups', 'seq'), None, 'chan'), parts along dimension 0
- dec_grad: bfloat16 [1536, 5, 1536], P(('groups', 'seq'), None, 'chan'), parts along dimension 0
There are 2 independent parts, one for each index of `groups`. A program takes and returns all parts, laid end to end along the dimension named above; an argument that names none is the same for every part. Nothing has to cross between parts.
All inputs are finite; a program needn't handle non-finite values.
Results may differ from a plain program's by a relative error of at most 0.012.
Values may be sent and summed in bfloat16 or wider, within the bound.
A program may use at most 128 MiB of HBM per device.

v0:
```python
import jax
import jax.numpy as jnp
from jax import lax
from jax.sharding import PartitionSpec as P


def with_halo(array, sides, width):
    for axis, dim in sides:
        size, length = (lax.axis_size(axis), array.shape[dim])
        up = [(i, (i + 1) % size) for i in range(size - 1)]
        down = [(j, i) for i, j in up]
        last = lax.slice_in_dim(array, length - width, length, axis=dim)
        first = lax.slice_in_dim(array, 0, width, axis=dim)
        before = lax.ppermute(last, axis, up)
        after = lax.ppermute(first, axis, down)
        array = jnp.concatenate([before, array, after], axis=dim)
    return array


def gelu_fn(values):
    return jax.nn.gelu(values, approximate=True)


def shards(inputs, enc_weight, dec_weight, cotangent):
    row_count = inputs.shape[0]
    half_rows = row_count // 2
    fine_width = inputs.shape[1]
    share_width = cotangent.shape[1]
    taps = enc_weight.shape[1]
    coarse_share = enc_weight.shape[2]
    contract_last = (((1,), (1,)), ((), ()))
    enc_full = lax.all_gather(enc_weight, "seq", axis=0, tiled=True)
    dec_full = lax.all_gather(dec_weight, "seq", axis=0, tiled=True)
    pooled = (
        inputs.astype(jnp.float32).reshape(half_rows, 2, fine_width).sum(axis=1) * 0.5
    ).astype(jnp.bfloat16)
    pad_pool = with_halo(pooled, (("seq", 0),), 2)
    pre_act = jnp.zeros((half_rows, coarse_share), jnp.float32)
    for tap_index in range(taps):
        pre_act = pre_act + jnp.dot(
            pad_pool[tap_index : tap_index + half_rows],
            enc_full[:, tap_index, :],
            preferred_element_type=jnp.float32,
        )
    hidden = gelu_fn(pre_act).astype(jnp.bfloat16)
    pad_hidden = with_halo(hidden, (("seq", 0),), 1)
    pad_up = jnp.repeat(pad_hidden, 2, axis=0)
    dec_part = jnp.zeros((row_count, fine_width), jnp.float32)
    for tap_index in range(taps):
        dec_part = dec_part + lax.dot_general(
            pad_up[tap_index : tap_index + row_count],
            dec_full[:, tap_index, :],
            contract_last,
            preferred_element_type=jnp.float32,
        )
    dec_share = lax.psum_scatter(
        dec_part.astype(jnp.bfloat16), "chan", scatter_dimension=1, tiled=True
    ).astype(jnp.float32)
    col_start = lax.axis_index("chan") * share_width
    skip_cols = lax.dynamic_slice_in_dim(inputs, col_start, share_width, 1)
    mixed_out = (skip_cols.astype(jnp.float32) + dec_share).astype(jnp.bfloat16)
    cot_full = lax.all_gather(cotangent, "chan", axis=1, tiled=True)
    pad_cot = with_halo(cot_full, (("seq", 0),), 2)
    up_grad = jnp.zeros((row_count, coarse_share), jnp.float32)
    for tap_index in range(taps):
        up_grad = up_grad + jnp.dot(
            pad_cot[4 - tap_index : 4 - tap_index + row_count],
            dec_full[:, tap_index, :],
            preferred_element_type=jnp.float32,
        )
    hid_grad = up_grad.reshape(half_rows, 2, coarse_share).sum(axis=1)
    _, pullback = jax.vjp(gelu_fn, pre_act)
    pre_grad = pullback(hid_grad)[0].astype(jnp.bfloat16)
    pad_grad = with_halo(pre_grad, (("seq", 0),), 2)
    pool_grad = jnp.zeros((half_rows, fine_width), jnp.float32)
    for tap_index in range(taps):
        pool_grad = pool_grad + lax.dot_general(
            pad_grad[4 - tap_index : 4 - tap_index + half_rows],
            enc_full[:, tap_index, :],
            contract_last,
            preferred_element_type=jnp.float32,
        )
    total_sum = lax.psum(pool_grad.astype(jnp.bfloat16), "chan").astype(jnp.float32)
    grad_share = lax.dynamic_slice_in_dim(total_sum, col_start, share_width, 1)
    input_grad = (cotangent.astype(jnp.float32) + 0.5 * jnp.repeat(grad_share, 2, axis=0)).astype(
        jnp.bfloat16
    )

    def dec_terms():
        return jnp.stack(
            [
                jnp.dot(
                    cot_full.T,
                    pad_up[tap_index : tap_index + row_count],
                    preferred_element_type=jnp.float32,
                )
                for tap_index in range(taps)
            ],
            axis=1,
        )

    joint_sum = lax.psum_scatter(
        jnp.concatenate(
            [
                jnp.stack(
                    [
                        jnp.dot(
                            pad_pool[tap_index : tap_index + half_rows].T,
                            pre_grad,
                            preferred_element_type=jnp.float32,
                        )
                        for tap_index in range(taps)
                    ],
                    axis=1,
                ),
                dec_terms(),
            ],
            axis=2,
        ).astype(jnp.bfloat16),
        "seq",
        scatter_dimension=0,
        tiled=True,
    ).astype(jnp.float32)
    enc_sum = joint_sum[:, :, :coarse_share]
    dec_sum = joint_sum[:, :, coarse_share:]
    return (mixed_out, input_grad, enc_sum.astype(jnp.bfloat16), dec_sum.astype(jnp.bfloat16))


def solution(mesh):
    return jax.shard_map(
        shards,
        mesh=mesh,
        in_specs=(
            P(("groups", "seq"), None),
            P("seq", None, "chan"),
            P("seq", None, "chan"),
            P(("groups", "seq"), "chan"),
        ),
        out_specs=(
            P(("groups", "seq"), "chan"),
            P(("groups", "seq"), "chan"),
            P(("groups", "seq"), None, "chan"),
            P(("groups", "seq"), None, "chan"),
        ),
        check_vma=False,
    )
```

profile of v0, /device:TPU:0, one launch (start us, length us, event | category | flops | bytes accessed | tf_op | source)
XLA Modules:
  0.0 509.0 jit_solution(5221697619440300852)
XLA Ops:
  8.7 2.7 all_gather.11
  12.7 5.4 %collective-permute-start.5 = (bf16[2,768]{1,0:T(2,128)(2,1)S(1)}, bf16[2,768]{1,0:T(2,128)(2,1)S(1)}, u32[]{:S(2)}, u32[]{:S(2)}) collective-permute-start(bf16[2,768]{1,0:T(2,128)(2,1)S(1)} %get-tuple-element.17), channel_id=1, source_target_pairs={{0,2},{2,4},{4,6},{6,8},{8,10},{10,12},{12,14},{1,3},{3,5},{5,7},{... | collective-permute-start | bytes 9224 | tf_op jit(solution)/shard_map/ppermute | solution.py:14
  18.9 1.9 reduce_sum.18
  20.8 4.8 collective-permute-start
  27.2 80.0 %all-gather.5.cloned.1.call-done = bf16[768,5,768]{2,0,1:T(8,128)(2,1)} async-done(((bf16[96,5,768]{2,0,1:T(8,128)(2,1)}), bf16[768,5,768]{2,0,1:T(8,128)(2,1)}) %all-gather.5.cloned.1.call-update) | async-done | bytes 5898256 | tf_op jit(solution)/shard_map/all_gather | solution.py:33
  107.2 2.2 fusion.37
  109.4 2.1 fusion.33
  113.1 2.1 add_add_fusion
  115.2 86.7 %all-gather.3.cloned.1.call-done = bf16[768,5,768]{2,0,1:T(8,128)(2,1)} async-done(((bf16[96,5,768]{2,0,1:T(8,128)(2,1)}), bf16[768,5,768]{2,0,1:T(8,128)(2,1)}) %all-gather.3.cloned.1.call-update) | async-done | bytes 5898256 | tf_op jit(solution)/shard_map/all_gather | solution.py:32
  203.6 2.6 fusion.30
  206.3 2.2 reshape.29
  208.5 2.9 reduce_sum.19
  213.2 1.9 fusion.23
  215.1 2.2 fusion.48
  219.8 4.5 collective-permute-start.7
  224.4 3.4 collective-permute-start.2
  231.5 2.7 fusion.27
  234.2 3.2 fusion.36
  238.5 2.5 copy-done
  245.2 2.4 fusion.38
  247.7 2.2 fusion.34
  249.9 2.2 fusion.32
  252.2 2.3 add_convert_fusion
  254.5 1.9 fusion.1
  261.1 3.1 fusion.3
  265.3 1.9 fusion.5
  269.1 1.9 fusion.9
  271.0 10.2 %pad_maximum_fusion = bf16[768,5,1536]{0,2,1:T(8,128)(2,1)} fusion(bf16[768,5,768]{0,2,1:T(8,128)(2,1)} %fusion.9, bf16[768,5,768]{0,2,1:T(8,128)(2,1)} %copy-done), kind=kLoop, calls=%fused_computation | loop fusion | flops 23592960 | bytes 23592960 | tf_op jit(solution)/shard_map/concatenate | solution.py:103
  281.2 16.4 %copy.16 = bf16[768,7680]{1,0:T(8,128)(2,1)} copy(bf16[768,7680]{0,1:T(8,128)(2,1)} %bitcast.119) | data formatting | bytes 23592960
  302.5 192.3 %reduce-scatter.9.cloned.1.call-done = bf16[96,7680]{1,0:T(8,128)(2,1)} async-done(((bf16[768,7680]{1,0:T(8,128)(2,1)}), bf16[96,7680]{1,0:T(8,128)(2,1)}) %reduce-scatter.9.cloned.1.call-update) | async-done | bytes 1474576
  494.8 2.7 copy.17
  499.0 2.3 copy.11
  (103 shorter events, 36.9 us)
Async XLA Ops:
  7.2 10.9 %copy-start.3 = (bf16[512,768]{1,0:T(8,128)(2,1)S(1)}, bf16[512,768]{1,0:T(8,128)(2,1)}, u32[]{:S(2)}) copy-start(bf16[512,768]{1,0:T(8,128)(2,1)} %param.4) | copy-start | bytes 2359300
  7.2 100.0 %all-gather.5.cloned.1.call-start = ((), (), s32[]{:S(2)}) async-start(), calls=%async_computation.3 | async-start | bytes 6635520 | tf_op jit(solution)/shard_map/all_gather | solution.py:33
  7.9 194.0 %all-gather.3.cloned.1.call-start = ((), (), s32[]{:S(2)}) async-start(), calls=%async_computation.2 | async-start | bytes 6635520 | tf_op jit(solution)/shard_map/all_gather | solution.py:32
  8.7 289.0 %all-reduce.2.cloned.1.call-start = ((), (), s32[]{:S(2)}) async-start(), calls=%async_computation.4 | async-start | bytes 786432 | tf_op jit(solution)/shard_map/psum | solution.py:83
  11.4 15.8 %collective-permute-start.4 = (bf16[2,768]{1,0:T(2,128)(2,1)S(1)}, bf16[2,768]{1,0:T(2,128)(2,1)S(1)}, u32[]{:S(2)}, u32[]{:S(2)}) collective-permute-start(bf16[2,768]{1,0:T(2,128)(2,1)S(1)} %get-tuple-element.16), channel_id=1, source_target_pairs={{2,0},{4,2},{6,4},{8,6},{10,8},{12,10},{14,12},{3,1},{5,3},{7,5},{... | collective-permute-start | bytes 9224 | tf_op jit(solution)/shard_map/ppermute | solution.py:15
  12.7 14.6 %collective-permute-start.5 = (bf16[2,768]{1,0:T(2,128)(2,1)S(1)}, bf16[2,768]{1,0:T(2,128)(2,1)S(1)}, u32[]{:S(2)}, u32[]{:S(2)}) collective-permute-start(bf16[2,768]{1,0:T(2,128)(2,1)S(1)} %get-tuple-element.17), channel_id=1, source_target_pairs={{0,2},{2,4},{4,6},{6,8},{8,10},{10,12},{12,14},{1,3},{3,5},{5,7},{... | collective-permute-start | bytes 9224 | tf_op jit(solution)/shard_map/ppermute | solution.py:14
  20.8 190.6 %collective-permute-start = (bf16[2,768]{1,0:T(2,128)(2,1)S(1)}, bf16[2,768]{1,0:T(2,128)(2,1)S(1)}, u32[]{:S(2)}, u32[]{:S(2)}) collective-permute-start(bf16[2,768]{1,0:T(2,128)(2,1)S(1)} %get-tuple-element.24), channel_id=1, source_target_pairs={{0,2},{2,4},{4,6},{6,8},{8,10},{10,12},{12,14},{1,3},{3,5},{5,7},{... | collective-permute-start | bytes 9224 | tf_op jit(solution)/shard_map/ppermute | solution.py:14
  25.7 178.0 %collective-permute-start.1 = (bf16[2,768]{1,0:T(2,128)(2,1)S(1)}, bf16[2,768]{1,0:T(2,128)(2,1)S(1)}, u32[]{:S(2)}, u32[]{:S(2)}) collective-permute-start(bf16[2,768]{1,0:T(2,128)(2,1)S(1)} %get-tuple-element.25), channel_id=1, source_target_pairs={{2,0},{4,2},{6,4},{8,6},{10,8},{12,10},{14,12},{3,1},{5,3},{7,5},{... | collective-permute-start | bytes 9224 | tf_op jit(solution)/shard_map/ppermute | solution.py:15
  107.2 4.3 copy-start.7
  203.6 11.5 %copy-start.14 = (bf16[2,768]{1,0:T(2,128)(2,1)}, bf16[2,768]{1,0:T(2,128)(2,1)S(1)}, u32[]{:S(2)}) copy-start(bf16[2,768]{1,0:T(2,128)(2,1)S(1)} %collective-permute-done.1) | copy-start | bytes 9220
  213.2 1.9 copy-start.10
  213.2 1.9 copy-start.16
  218.5 38.4 %collective-permute-start.6 = (bf16[2,768]{1,0:T(2,128)(2,1)}, bf16[2,768]{1,0:T(2,128)(2,1)}, u32[]{:S(2)}, u32[]{:S(2)}) collective-permute-start(bf16[2,768]{1,0:T(2,128)(2,1)} %get-tuple-element.18), channel_id=1, source_target_pairs={{2,0},{4,2},{6,4},{8,6},{10,8},{12,10},{14,12},{3,1},{5,3},{7,5},{... | collective-permute-start | bytes 9224 | tf_op jit(solution)/shard_map/ppermute | solution.py:15
  219.8 36.6 %collective-permute-start.7 = (bf16[2,768]{1,0:T(2,128)(2,1)}, bf16[2,768]{1,0:T(2,128)(2,1)S(1)}, u32[]{:S(2)}, u32[]{:S(2)}) collective-permute-start(bf16[2,768]{1,0:T(2,128)(2,1)} %get-tuple-element.19), channel_id=1, source_target_pairs={{0,2},{2,4},{4,6},{6,8},{8,10},{10,12},{12,14},{1,3},{3,5},{5,7},{... | collective-permute-start | bytes 9224 | tf_op jit(solution)/shard_map/ppermute | solution.py:14
  224.4 16.6 %collective-permute-start.2 = (bf16[1,768]{1,0:T(2,128)(2,1)}, bf16[1,768]{1,0:T(2,128)(2,1)S(1)}, u32[]{:S(2)}, u32[]{:S(2)}) collective-permute-start(bf16[1,768]{1,0:T(2,128)(2,1)} %get-tuple-element.22), channel_id=1, source_target_pairs={{0,2},{2,4},{4,6},{6,8},{8,10},{10,12},{12,14},{1,3},{3,5},{5,7},{... | collective-permute-start | bytes 4616 | tf_op jit(solution)/shard_map/ppermute | solution.py:14
  227.7 13.3 %collective-permute-start.3 = (bf16[1,768]{1,0:T(2,128)(2,1)}, bf16[1,768]{1,0:T(2,128)(2,1)S(1)}, u32[]{:S(2)}, u32[]{:S(2)}) collective-permute-start(bf16[1,768]{1,0:T(2,128)(2,1)} %get-tuple-element.23), channel_id=1, source_target_pairs={{2,0},{4,2},{6,4},{8,6},{10,8},{12,10},{14,12},{3,1},{5,3},{7,5},{... | collective-permute-start | bytes 4616 | tf_op jit(solution)/shard_map/ppermute | solution.py:15
  230.0 4.2 copy-start.11
  234.2 3.2 copy-start.15
  238.5 2.5 copy-start
  245.2 2.4 copy-start.8
  247.7 2.3 copy-start.13
  247.7 4.5 copy-start.6
  249.9 6.4 %slice-start = ((s8[5898240]{0:T(1024)(128)(4,1)}), s8[4194304]{0:T(1024)(128)(4,1)S(1)}, s32[]{:S(2)}) async-start(s8[5898240]{0:T(1024)(128)(4,1)} %bitcast.121), calls=%async_computation.7 | async-start | bytes 8388608
  252.2 4.2 slice-start.1
  256.9 1.3 copy-start.2
  260.8 4.6 copy-start.12
  260.8 39.6 %reduce-scatter.7.cloned.1.call-start = ((), (), s32[]{:S(2)}) async-start(), calls=%async_computation.5 | async-start | bytes 1179648
  265.3 1.9 copy-start.9
  267.2 227.6 %reduce-scatter.9.cloned.1.call-start = ((), (), s32[]{:S(2)}) async-start(), calls=%async_computation.6 | async-start | bytes 13271040
  297.7 1.9 copy-start.5
  299.0 2.6 copy-start.4
  499.0 2.3 copy-start.1
Sparse Core Ops, SparseCore 0:
  10.2 96.9 all-gather.4
  109.4 92.4 all-gather.2
  260.9 19.2 all-reduce.1
  282.3 9.3 reduce-scatter.6
  297.8 196.9 reduce-scatter.8
where the time goes:
time: 510 us; the launch traced here: 509 us
  waiting for transfers between devices  360 us (71%)
  matrix products  50.6 us (10%)
  local copies, waits for them, and re-layouts  38.8 us (8%)
  starting transfers between devices  24.2 us (5%)
  other arithmetic  18 us (4%)
  between operations  14.4 us (3%)
    unnamed x7, waiting for transfers between devices  194 us
    all_gather x1, waiting for transfers between devices, shards(): enc_full = lax.all_gather(enc_weight, 'seq', axis=0, tiled=True)  86.7 us
    all_gather x1, waiting for transfers between devices, shards(): dec_full = lax.all_gather(dec_weight, 'seq', axis=0, tiled=True)  80 us
    unnamed x45, local copies, waits for them, and re-layouts  27.7 us
    ppermute x4, starting transfers between devices, with_halo(): before = lax.ppermute(last, axis, up)  18.1 us
    dot_general x5, matrix products, shards(): lax.dot_general(pad_up[tap_index:tap_index + row_count], dec_full[:, tap_...  12.4 us
    dot_general x5, matrix products, dec_terms(): jnp.dot(cot_full.T, pad_up[tap_index:tap_index + row_count], preferred_el...  10.5 us
    dot_general x5, matrix products, shards(): jnp.dot(pad_pool[tap_index:tap_index + half_rows], enc_full[:, tap_index,...  10.2 us
  transfers between devices with their start and end apart: 13, of which 3 were waited for; matrix products, arithmetic and copies ran while one was open for 17% of the time, Pallas kernels for 0%

commit v1 on v0

v1 whole, which is shorter than its diff:
```python
import jax
import jax.numpy as jnp
from jax import lax
from jax.sharding import PartitionSpec as P

BF16 = jnp.bfloat16
F32 = jnp.float32


def shift(array, by):
    length = array.shape[0]
    if by == 0:
        return array
    pad = jnp.zeros((abs(by),) + array.shape[1:], array.dtype)
    if by > 0:
        return jnp.concatenate([array[by:], pad], axis=0)
    return jnp.concatenate([pad, array[: length + by]], axis=0)


def to_columns(array, parts):
    rows, cols = array.shape
    blocks = array.reshape(rows, parts, cols // parts).transpose(1, 0, 2)
    return lax.all_to_all(blocks, "seq", 0, 0, tiled=True)


def to_rows(blocks):
    parts, rows, cols = blocks.shape
    got = lax.all_to_all(blocks, "seq", 0, 0, tiled=True)
    return got.transpose(1, 0, 2).reshape(rows, parts * cols)


def gelu_fn(values):
    return jax.nn.gelu(values, approximate=True)


def shards(inputs, enc_weight, dec_weight, cotangent):
    parts = lax.axis_size("seq")
    rows, width = inputs.shape
    half = rows // 2
    total = half * parts
    block, taps, share = enc_weight.shape
    half_width = cotangent.shape[1]

    pooled = (inputs.astype(F32).reshape(half, 2, width).sum(axis=1) * 0.5).astype(BF16)
    cot_full = lax.all_gather(cotangent, "chan", axis=1, tiled=True)
    columns = to_columns(jnp.concatenate([pooled, cot_full], axis=0), parts)
    pool_col = columns[:, :half].reshape(total, block)
    cot_col = columns[:, half:].reshape(total, 2, block).astype(F32)
    even = cot_col[:, 0]
    odd = cot_col[:, 1]
    pair = (even + odd).astype(BF16)
    cross = (odd + shift(even, 1)).astype(BF16)
    before = jnp.concatenate([even[:1].astype(BF16), cross[:-1]], axis=0)
    pool_taps = jnp.concatenate([shift(pool_col, t - 2) for t in range(taps)], axis=1)
    cot_taps = jnp.concatenate([shift(pair, 1), cross, pair, before, shift(pair, -1)], axis=1)
    enc_mat = enc_weight.transpose(1, 0, 2).reshape(taps * block, share)
    dec_mat = dec_weight.transpose(1, 0, 2).reshape(taps * block, share)

    partial = jnp.concatenate(
        [
            jnp.dot(pool_taps, enc_mat, preferred_element_type=F32).astype(BF16),
            jnp.dot(cot_taps, dec_mat, preferred_element_type=F32).astype(BF16),
        ],
        axis=1,
    )
    summed = lax.psum_scatter(partial, "seq", scatter_dimension=0, tiled=True).astype(F32)
    pre_act = summed[:, :share]
    hid_grad = summed[:, share:]
    hidden, pullback = jax.vjp(gelu_fn, pre_act)
    pre_grad = pullback(hid_grad)[0].astype(BF16)
    joint = jnp.concatenate([hidden.astype(BF16), pre_grad], axis=1)
    joint = lax.all_gather(joint, "seq", axis=0, tiled=True)
    hidden_all = joint[:, :share]
    grad_all = joint[:, share:]

    contract_rows = (((0,), (0,)), ((), ()))
    contract_last = (((1,), (1,)), ((), ()))
    dec_grad = lax.dot_general(cot_taps, hidden_all, contract_rows, preferred_element_type=F32)
    enc_grad = lax.dot_general(pool_taps, grad_all, contract_rows, preferred_element_type=F32)
    dec_grad = dec_grad.astype(BF16).reshape(taps, block, share).transpose(1, 0, 2)
    enc_grad = enc_grad.astype(BF16).reshape(taps, block, share).transpose(1, 0, 2)

    dec_out = lax.dot_general(hidden_all, dec_mat, contract_last, preferred_element_type=F32)
    p0, p1, p2, p3, p4 = [dec_out[:, t * block : (t + 1) * block] for t in range(taps)]
    after4 = shift(p4, 1)
    before0 = shift(p0, -1)
    dec_even = before0 + shift(p1, -1) + p2 + p3 + after4
    dec_odd = before0 + p1 + p2 + shift(p3, 1) + after4
    decoded = jnp.stack([dec_even, dec_odd], axis=1).astype(BF16).reshape(parts, rows, block)
    enc_out = lax.dot_general(grad_all, enc_mat, contract_last, preferred_element_type=F32)
    pool_grad = sum(shift(enc_out[:, t * block : (t + 1) * block], 2 - t) for t in range(taps))
    pool_grad = pool_grad.astype(BF16).reshape(parts, half, block)
    mine = to_rows(jnp.concatenate([decoded, pool_grad], axis=1))
    mine = lax.psum_scatter(mine, "chan", scatter_dimension=1, tiled=True).astype(F32)

    col_start = lax.axis_index("chan") * half_width
    skip = lax.dynamic_slice_in_dim(inputs, col_start, half_width, 1)
    mixed_out = (skip.astype(F32) + mine[:rows]).astype(BF16)
    input_grad = (cotangent.astype(F32) + 0.5 * jnp.repeat(mine[rows:], 2, axis=0)).astype(BF16)
    return mixed_out, input_grad, enc_grad, dec_grad


def solution(mesh):
    return jax.shard_map(
        shards,
        mesh=mesh,
        in_specs=(
            P(("groups", "seq"), None),
            P("seq", None, "chan"),
            P("seq", None, "chan"),
            P(("groups", "seq"), "chan"),
        ),
        out_specs=(
            P(("groups", "seq"), "chan"),
            P(("groups", "seq"), "chan"),
            P(("groups", "seq"), None, "chan"),
            P(("groups", "seq"), None, "chan"),
        ),
        check_vma=False,
    )
```

time: 510 us -> 362 us (0.71)
  waiting for transfers between devices: 360 us -> 216 us
  blocking collectives: 2.66 us -> 70.8 us
  matrix products: 50.6 us -> 23.9 us
  starting transfers between devices: 24.2 us -> 0.3 us
  local copies, waits for them, and re-layouts: 38.8 us -> 22.7 us
    unnamed x7 -> x3, waiting for transfers between devices: 194 us -> 0.05 us
    reduce_scatter x0 -> x2, waiting for transfers between devices: none -> 117 us  [the longest x1 117 us: shards(): lax.psum_scatter(partial, 'seq', scatter_dimension=0, tiled=True)]
    all_to_all x0 -> x2, blocking collectives: none -> 68.2 us  [the longest x1 36.2 us: to_columns(): return lax.all_to_all(blocks, 'seq', 0, 0, tiled=True)]
    all_gather x2 -> x1, waiting for transfers between devices: 167 us -> 99.2 us  [shards(): joint = lax.all_gather(joint, 'seq', axis=0, tiled=True)]
    dot_general x30 -> x6, matrix products: 50.6 us -> 23.9 us  [the longest x1 4.87 us: shards(): lax.dot_general(cot_taps, hidden_all, contract_rows, preferred_element_ty...]
    ppermute x8 -> x0, starting transfers between devices: 23.7 us -> none  [the longest x4 18.1 us: with_halo(): before = lax.ppermute(last, axis, up)]
    unnamed x45 -> x38, local copies, waits for them, and re-layouts: 27.7 us -> 6.97 us
    concatenate x1 -> x5, local copies, waits for them, and re-layouts: 0.01 us -> 6.21 us  [the longest x1 5.21 us: shards(): jnp.concatenate([shift(pair, 1), cross, pair, before, shift(pair, -1)], a...]
  transfers between devices with their start and end apart: 13 -> 3, of which waited for: 3 -> 2; matrix products, arithmetic and copies ran while one was open for 17% -> 3% of each run, Pallas kernels for 0% -> 0%
where the time goes in v1:
time: 362 us; the launch traced here: 361 us
  waiting for transfers between devices  216 us (60%)
  blocking collectives  70.8 us (20%)
  matrix products  23.9 us (7%)
  local copies, waits for them, and re-layouts  22.7 us (6%)
  between operations  14.2 us (4%)
  other arithmetic  13.2 us (4%)
    reduce_scatter x1, waiting for transfers between devices, shards(): lax.psum_scatter(partial, 'seq', scatter_dimension=0, tiled=True)  117 us
    all_gather x1, waiting for transfers between devices, shards(): joint = lax.all_gather(joint, 'seq', axis=0, tiled=True)  99.2 us
    all_to_all x1, blocking collectives, to_columns(): return lax.all_to_all(blocks, 'seq', 0, 0, tiled=True)  36.2 us
    all_to_all x1, blocking collectives, to_rows(): got = lax.all_to_all(blocks, 'seq', 0, 0, tiled=True)  32 us
  transfers between devices with their start and end apart: 3, of which 2 were waited for; matrix products, arithmetic and copies ran while one was open for 3% of the time, Pallas kernels for 0%

profile of v1, /device:TPU:0, one launch (start us, length us, event | category | flops | bytes accessed | tf_op | source)
XLA Modules:
  0.0 361.4 jit_solution(7781944280728528370)
XLA Ops:
  7.2 1.3 copy.36
  8.5 2.6 all_gather.6
  11.1 0.8 reshape.73
  11.9 1.9 reduce_sum.9
  14.1 0.8 copy-done.2
  15.0 36.2 %all_to_all.10 = bf16[8,768,96]{1,2,0:T(8,128)(2,1)S(1)} all-to-all(bf16[8,768,96]{1,2,0:T(8,128)(2,1)S(1)} %bitcast.56), channel_id=1, replica_groups=mesh['groups'=2,'seq'=8,'chan'=2] {'seq'}, dimensions={0} | all-to-all | bytes 2359296 | tf_op jit(solution)/shard_map/all_to_all | solution.py:23
  51.2 1.0 fusion.39
  52.2 1.0 fusion.38
  53.3 0.7 copy.38
  54.0 0.8 slice.155
  54.8 1.5 fusion.36
  58.0 1.0 pad_maximum_fusion.5
  59.0 1.3 copy-done.12
  60.3 3.5 convolution_convert_fusion.1
  63.9 5.2 %concatenate.76 = bf16[2048,480]{1,0:T(8,128)(2,1)} concatenate(bf16[2048,96]{1,0:T(8,128)(2,1)S(1)} %concatenate.72, bf16[2048,96]{1,0:T(8,128)(2,1)S(1)} %get-tuple-element.28, bf16[2048,96]{1,0:T(8,128)(2,1)S(1)} %get-tuple-element.29, bf16[2048,96]{1,0:T(8,128)(2,1)} %pad_maximum_fusion.5, bf16[2048,96]{1,0:T(8,128)(2,1)S(1)} %concatenate.75), dimensions={1} | concatenate | bytes 3932160 | tf_op jit(solution)/shard_map/concatenate | solution.py:55
  69.1 3.7 %convolution_convert_fusion = bf16[2048,768]{0,1:T(8,128)(2,1)S(1)} fusion(bf16[2048,480]{1,0:T(8,128)(2,1)} %concatenate.76, bf16[480,768]{1,0:T(8,128)(2,1)} %bitcast.63), kind=kOutput, calls=%fused_computation.1 | convolution fusion | flops 1511522304 | bytes 5849088 | tf_op jit(solution)/shard_map/dot_general | solution.py:62
  72.8 3.8 %pad_maximum_fusion = bf16[2048,1536]{0,1:T(8,128)(2,1)} fusion(bf16[2048,768]{0,1:T(8,128)(2,1)S(1)} %convolution_convert_fusion, bf16[2048,768]{0,1:T(8,128)(2,1)S(1)} %copy-done.3), kind=kLoop, calls=%fused_computation | loop fusion | flops 12582912 | bytes 12582912 | tf_op jit(solution)/shard_map/concatenate | solution.py:59
  76.9 117.0 %reduce-scatter.3.cloned.1.call-done = bf16[256,1536]{0,1:T(8,128)(2,1)} async-done(((bf16[2048,1536]{0,1:T(8,128)(2,1)}), bf16[256,1536]{0,1:T(8,128)(2,1)}) %reduce-scatter.3.cloned.1.call-update) | async-done | bytes 786448 | tf_op jit(solution)/shard_map/reduce_scatter | solution.py:66
  193.8 1.2 convert_element_type.81
  195.7 0.9 pad_maximum_fusion.3
  196.7 99.2 %all-gather.2.cloned.1.call-done = bf16[2048,1536]{0,1:T(8,128)(2,1)} async-done(((bf16[256,1536]{0,1:T(8,128)(2,1)}), bf16[2048,1536]{0,1:T(8,128)(2,1)}) %all-gather.2.cloned.1.call-update) | async-done | bytes 6291472 | tf_op jit(solution)/shard_map/all_gather | solution.py:72
  295.9 3.6 fusion.2
  301.1 3.6 fusion.6
  305.9 0.8 copy.42
  307.0 0.7 copy.44
  307.7 32.0 %all_to_all.11 = bf16[8,768,96]{1,2,0:T(8,128)(2,1)} all-to-all(bf16[8,768,96]{1,2,0:T(8,128)(2,1)S(1)} %copy.44), channel_id=1, replica_groups=mesh['groups'=2,'seq'=8,'chan'=2] {'seq'}, dimensions={0} | all-to-all | bytes 2359296 | tf_op jit(solution)/shard_map/all_to_all | solution.py:28
  340.0 1.3 copy-done.13
  341.3 4.6 %fusion.11 = bf16[480,768]{1,0:T(8,128)(2,1)} fusion(bf16[2048,480]{0,1:T(8,128)(2,1)S(1)} %copy-done.13, bf16[2048,1536]{0,1:T(8,128)(2,1)} %all-gather.2.cloned.1.call-done), kind=kOutput, calls=%fused_computation.13 | convolution fusion | flops 1510318080 | bytes 5849088 | tf_op jit(solution)/shard_map/dot_general | solution.py:79
  345.9 4.9 %fusion.8 = bf16[480,768]{1,0:T(8,128)(2,1)} fusion(bf16[2048,480]{1,0:T(8,128)(2,1)S(1)} %copy-done.4, bf16[2048,1536]{0,1:T(8,128)(2,1)} %all-gather.2.cloned.1.call-done), kind=kOutput, calls=%fused_computation.12 | convolution fusion | flops 1510318080 | bytes 5849088 | tf_op jit(solution)/shard_map/dot_general | solution.py:78
  350.8 1.1 convert_element_type.86
  352.3 0.9 copy.46
  354.0 0.8 add_convert_fusion.2
  (67 shorter events, 7.6 us)
Async XLA Ops:
  7.2 51.8 %copy-start = (bf16[96,5,768]{2,0,1:T(8,128)(2,1)S(1)}, bf16[96,5,768]{2,0,1:T(8,128)(2,1)}, u32[]{:S(2)}) copy-start(bf16[96,5,768]{2,0,1:T(8,128)(2,1)} %param.5) | copy-start | bytes 2211844
  7.2 3.9 %copy-start.5 = (bf16[512,768]{1,0:T(8,128)(2,1)S(1)}, bf16[512,768]{1,0:T(8,128)(2,1)}, u32[]{:S(2)}) copy-start(bf16[512,768]{1,0:T(8,128)(2,1)} %param.4) | copy-start | bytes 2359300
  7.2 186.6 %reduce-scatter.3.cloned.1.call-start = ((), (), s32[]{:S(2)}) async-start(), calls=%async_computation.4 | async-start | bytes 7077888 | tf_op jit(solution)/shard_map/reduce_scatter | solution.py:66
  13.7 1.1 copy-start.2
  56.5 1.0 copy-start.11
  56.6 1.2 copy-start.10
  57.0 2.0 copy-start.9
  57.5 1.4 copy-start.8
  59.0 1.3 copy-start.12
  69.1 3.7 %copy-start.3 = (bf16[2048,768]{0,1:T(8,128)(2,1)S(1)}, bf16[2048,768]{0,1:T(8,128)(2,1)}, u32[]{:S(2)}) copy-start(bf16[2048,768]{0,1:T(8,128)(2,1)} %convolution_convert_fusion.1) | copy-start | bytes 9437188
  76.6 219.2 %all-gather.2.cloned.1.call-start = ((), (), s32[]{:S(2)}) async-start(), calls=%async_computation.5 | async-start | bytes 7077888 | tf_op jit(solution)/shard_map/all_gather | solution.py:72
  196.6 154.2 %reduce-scatter.5.cloned.1.call-start = ((), (), s32[]{:S(2)}) async-start(), calls=%async_computation.6 | async-start | bytes 1769472 | tf_op jit(solution)/shard_map/reduce_scatter | solution.py:94
  300.0 1.1 copy-start.14
  307.7 32.1 %copy-start.6 = (bf16[512,768]{1,0:T(8,128)(2,1)S(1)}, bf16[512,768]{1,0:T(8,128)(2,1)}, u32[]{:S(2)}) copy-start(bf16[512,768]{1,0:T(8,128)(2,1)} %param.4) | copy-start | bytes 2359300
  339.7 1.5 copy-start.13
  341.3 4.6 %copy-start.4 = (bf16[2048,480]{1,0:T(8,128)(2,1)S(1)}, bf16[2048,480]{1,0:T(8,128)(2,1)}, u32[]{:S(2)}) copy-start(bf16[2048,480]{1,0:T(8,128)(2,1)} %concatenate.76) | copy-start | bytes 5898244
  352.1 1.9 copy-start.7
  352.3 2.6 copy-start.1
Sparse Core Ops, SparseCore 0:
  76.8 117.0 reduce-scatter.2
  196.7 99.0 all-gather.1
  339.9 7.3 reduce-scatter.4

commit v2 on v1

--- a/solution.py
+++ b/solution.py
@@ -1,6 +1,11 @@
+import functools
+import math
+
 import jax
 import jax.numpy as jnp
 from jax import lax
+from jax.experimental import pallas as pl
+from jax.experimental.pallas import tpu as pltpu
 from jax.sharding import PartitionSpec as P
 
 BF16 = jnp.bfloat16
@@ -29,8 +34,191 @@
     return got.transpose(1, 0, 2).reshape(rows, parts * cols)
 
 
-def gelu_fn(values):
-    return jax.nn.gelu(values, approximate=True)
+PIECES = 2
+
+
+def ring_place(index, n):
+    if n != 8:
+        return index
+    y = lax.rem(index, 2)
+    z = index // 2
+    return z + y * (n - 1 - 2 * z)
+
+
+def ring_index(place, n):
+    place = lax.rem(place + 2 * n, n)
+    if n != 8:
+        return place
+    back = place // (n // 2)
+    return 2 * place + back * (2 * n - 1 - 4 * place)
+
+
+def gelu_and_slope(v):
+    scale = math.sqrt(2.0 / math.pi)
+    square = v * v
+    th = jnp.tanh(scale * (v + 0.044715 * square * v))
+    up = 0.5 * (1.0 + th)
+    slope = up + 0.5 * v * (1.0 - th * th) * (scale * (1.0 + 3.0 * 0.044715 * square))
+    return v * up, slope
+
+
+def ring_kernel(
+    n, x_ref, y_ref, enc_ref, dec_ref, out_ref, slots, term, mine,
+    rs_send, rs_recv, ag_send, ag_recv, local_sem,
+):
+    me = lax.axis_index("seq")
+    place = ring_place(me, n)
+    nexts = (ring_index(place + 1, n), ring_index(place - 1, n))
+    half = x_ref.shape[1]
+    share = enc_ref.shape[1]
+    side = half // 2
+    piece = side // PIECES
+
+    barrier = pltpu.get_barrier_semaphore()
+    for other in nexts:
+        pl.semaphore_signal(
+            barrier, inc=1, device_id={"seq": other}, device_id_type=pl.DeviceIdType.MESH
+        )
+    pl.semaphore_wait(barrier, 2)
+
+    def signed(d, steps):
+        return place - steps if d == 0 else place + steps
+
+    def own_term(d, steps):
+        chunk = ring_index(signed(d, steps), n)
+        at = pl.ds(d * side, side)
+        a = jnp.dot(x_ref[chunk, at, :], enc_ref[...], preferred_element_type=jnp.float32)
+        b = jnp.dot(y_ref[chunk, at, :], dec_ref[...], preferred_element_type=jnp.float32)
+        return a, b
+
+    def rs_copy(d, s, q):
+        at = pl.ds(q * piece, piece)
+        return pltpu.make_async_remote_copy(
+            src_ref=slots.at[d, s, at],
+            dst_ref=slots.at[d, s + 1, at],
+            send_sem=rs_send.at[d, s, q],
+            recv_sem=rs_recv.at[d, s, q],
+            device_id={"seq": nexts[d]},
+            device_id_type=pl.DeviceIdType.MESH,
+        )
+
+    def ag_copy(d, s, q, first):
+        at = pl.ds(d * side + q * piece, piece)
+        owner = ring_index(signed(d, s), n)
+        return pltpu.make_async_remote_copy(
+            src_ref=mine.at[at] if first else out_ref.at[owner, at],
+            dst_ref=out_ref.at[owner, at],
+            send_sem=ag_send.at[d, s, q],
+            recv_sem=ag_recv.at[d, s, q],
+            device_id={"seq": nexts[d]},
+            device_id_type=pl.DeviceIdType.MESH,
+        )
+
+    for d in range(2):
+        a, b = own_term(d, 1)
+        slots[d, 0, :, :share] = a.astype(BF16)
+        slots[d, 0, :, share:] = b.astype(BF16)
+        for q in range(PIECES):
+            rs_copy(d, 0, q).start()
+
+    def fill(s):
+        for d in range(2):
+            a, b = own_term(d, s + 2)
+            term[d, :, :share] = a
+            term[d, :, share:] = b
+
+    def rs_step(s, carry):
+        fill(s)
+        for q in range(PIECES):
+            at = pl.ds(q * piece, piece)
+            for d in range(2):
+                rs_copy(d, s, q).wait_recv()
+                total = slots[d, s + 1, at, :].astype(F32) + term[d, at, :]
+                slots[d, s + 1, at, :] = total.astype(BF16)
+                rs_copy(d, s + 1, q).start()
+        return carry
+
+    lax.fori_loop(0, n - 2, rs_step, 0)
+    fill(n - 2)
+    for q in range(PIECES):
+        at = pl.ds(q * piece, piece)
+        for d in range(2):
+            rs_copy(d, n - 2, q).wait_recv()
+            rows = pl.ds(d * side + q * piece, piece)
+            pre = slots[d, n - 1, at, :share].astype(F32) + term[d, at, :share]
+            grad = slots[d, n - 1, at, share:].astype(F32) + term[d, at, share:]
+            value, slope = gelu_and_slope(pre)
+            mine[rows, :share] = value.astype(BF16)
+            mine[rows, share:] = (grad * slope).astype(BF16)
+            ag_copy(d, 0, q, True).start()
+    local = pltpu.make_async_copy(mine, out_ref.at[me], local_sem)
+    local.start()
+
+    def ag_step(s, carry):
+        for q in range(PIECES):
+            for d in range(2):
+                incoming(d, s, q).wait_recv()
+                ag_copy(d, s + 1, q, False).start()
+        return carry
+
+    def incoming(d, s, q):
+        at = pl.ds(d * side + q * piece, piece)
+        owner = ring_index(signed(d, s + 1), n)
+        return pltpu.make_async_remote_copy(
+            src_ref=mine.at[at],
+            dst_ref=out_ref.at[owner, at],
+            send_sem=ag_send.at[d, s, q],
+            recv_sem=ag_recv.at[d, s, q],
+            device_id={"seq": nexts[d]},
+            device_id_type=pl.DeviceIdType.MESH,
+        )
+
+    lax.fori_loop(0, n - 2, ag_step, 0)
+    for q in range(PIECES):
+        for d in range(2):
+            incoming(d, n - 2, q).wait_recv()
+
+    def drain(s, carry):
+        for q in range(PIECES):
+            for d in range(2):
+                rs_copy(d, s, q).wait_send()
+                ag_copy(d, s, q, True).wait_send()
+        return carry
+
+    lax.fori_loop(0, n - 1, drain, 0)
+    local.wait()
+
+
+def ring(pool_taps, cot_taps, enc_mat, dec_mat, n):
+    half = pool_taps.shape[1]
+    share = enc_mat.shape[1]
+    depth = enc_mat.shape[0]
+    vmem = pl.BlockSpec(memory_space=pltpu.VMEM)
+    steps = (2, n - 1, PIECES)
+    return pl.pallas_call(
+        functools.partial(ring_kernel, n),
+        out_shape=jax.ShapeDtypeStruct((n, half, 2 * share), BF16),
+        in_specs=[vmem] * 4,
+        out_specs=pl.BlockSpec(memory_space=pl.ANY),
+        scratch_shapes=[
+            pltpu.VMEM((2, n, half // 2, 2 * share), BF16),
+            pltpu.VMEM((2, half // 2, 2 * share), F32),
+            pltpu.VMEM((half, 2 * share), BF16),
+            pltpu.SemaphoreType.DMA(steps),
+            pltpu.SemaphoreType.DMA(steps),
+            pltpu.SemaphoreType.DMA(steps),
+            pltpu.SemaphoreType.DMA(steps),
+            pltpu.SemaphoreType.DMA,
+        ],
+        compiler_params=pltpu.CompilerParams(
+            collective_id=0, has_side_effects=True, vmem_limit_bytes=48 * 2**20
+        ),
+        cost_estimate=pl.CostEstimate(
+            flops=4 * n * half * depth * share,
+            bytes_accessed=4 * n * half * share * 2,
+            transcendentals=half * share,
+        ),
+    )(pool_taps, cot_taps, enc_mat, dec_mat)
 
 
 def shards(inputs, enc_weight, dec_weight, cotangent):
@@ -43,9 +231,20 @@
 
     pooled = (inputs.astype(F32).reshape(half, 2, width).sum(axis=1) * 0.5).astype(BF16)
     cot_full = lax.all_gather(cotangent, "chan", axis=1, tiled=True)
-    columns = to_columns(jnp.concatenate([pooled, cot_full], axis=0), parts)
-    pool_col = columns[:, :half].reshape(total, block)
-    cot_col = columns[:, half:].reshape(total, 2, block).astype(F32)
+    core = lax.axis_index("chan")
+    cores = lax.axis_size("chan")
+    few = half // cores
+    leaving = jnp.concatenate(
+        [
+            lax.dynamic_slice_in_dim(pooled, core * few, few, 0),
+            lax.dynamic_slice_in_dim(cot_full, core * 2 * few, 2 * few, 0),
+        ],
+        axis=0,
+    )
+    columns = to_columns(leaving, parts).reshape(parts, 1, 3 * few, block)
+    columns = lax.all_gather(columns, "chan", axis=1, tiled=True)
+    pool_col = columns[:, :, :few].reshape(total, block)
+    cot_col = columns[:, :, few:].reshape(total, 2, block).astype(F32)
     even = cot_col[:, 0]
     odd = cot_col[:, 1]
     pair = (even + odd).astype(BF16)
@@ -56,20 +255,13 @@
     enc_mat = enc_weight.transpose(1, 0, 2).reshape(taps * block, share)
     dec_mat = dec_weight.transpose(1, 0, 2).reshape(taps * block, share)
 
-    partial = jnp.concatenate(
-        [
-            jnp.dot(pool_taps, enc_mat, preferred_element_type=F32).astype(BF16),
-            jnp.dot(cot_taps, dec_mat, preferred_element_type=F32).astype(BF16),
-        ],
-        axis=1,
-    )
-    summed = lax.psum_scatter(partial, "seq", scatter_dimension=0, tiled=True).astype(F32)
-    pre_act = summed[:, :share]
-    hid_grad = summed[:, share:]
-    hidden, pullback = jax.vjp(gelu_fn, pre_act)
-    pre_grad = pullback(hid_grad)[0].astype(BF16)
-    joint = jnp.concatenate([hidden.astype(BF16), pre_grad], axis=1)
-    joint = lax.all_gather(joint, "seq", axis=0, tiled=True)
+    joint = ring(
+        pool_taps.reshape(parts, half, taps * block),
+        cot_taps.reshape(parts, half, taps * block),
+        enc_mat,
+        dec_mat,
+        parts,
+    ).reshape(total, 2 * share)
     hidden_all = joint[:, :share]
     grad_all = joint[:, share:]
 
@@ -90,10 +282,12 @@
     enc_out = lax.dot_general(grad_all, enc_mat, contract_last, preferred_element_type=F32)
     pool_grad = sum(shift(enc_out[:, t * block : (t + 1) * block], 2 - t) for t in range(taps))
     pool_grad = pool_grad.astype(BF16).reshape(parts, half, block)
-    mine = to_rows(jnp.concatenate([decoded, pool_grad], axis=1))
-    mine = lax.psum_scatter(mine, "chan", scatter_dimension=1, tiled=True).astype(F32)
-
-    col_start = lax.axis_index("chan") * half_width
+    mine = jnp.concatenate([decoded, pool_grad], axis=1)
+    mine = lax.psum_scatter(mine, "chan", scatter_dimension=1, tiled=True)
+    mine = lax.all_gather(to_rows(mine), "chan", axis=0, tiled=True)
+    col_start = core * half_width
+    mine = lax.dynamic_slice_in_dim(mine, col_start, half_width, 1).astype(F32)
+
     skip = lax.dynamic_slice_in_dim(inputs, col_start, half_width, 1)
     mixed_out = (skip.astype(F32) + mine[:rows]).astype(BF16)
     input_grad = (cotangent.astype(F32) + 0.5 * jnp.repeat(mine[rows:], 2, axis=0)).astype(BF16)

time: 362 us -> 276 us (0.76)
  waiting for transfers between devices: 216 us -> 16.5 us
  Pallas kernels: 0 us -> 124 us
  blocking collectives: 70.8 us -> 49.2 us
  local copies, waits for them, and re-layouts: 22.7 us -> 42.6 us
  matrix products: 23.9 us -> 14.6 us
    pallas_call x0 -> x1, Pallas kernels: none -> 124 us  [ring(): pl.pallas_call(functools.partial(ring_kernel, n), out_shape=jax.ShapeDtyp...]
    reduce_scatter x2 -> x1, waiting for transfers between devices: 117 us -> 8.92 us  [shards(): mine = lax.psum_scatter(mine, 'chan', scatter_dimension=1, tiled=True)]
    all_gather x1 -> x2, waiting for transfers between devices: 99.2 us -> 7.55 us  [the longest x1 7.55 us: shards(): columns = lax.all_gather(columns, 'chan', axis=1, tiled=True)]
    all_to_all x1, blocking collectives: 36.2 us -> 23.9 us  [to_columns(): return lax.all_to_all(blocks, 'seq', 0, 0, tiled=True)]
    concatenate x1 -> x2, local copies, waits for them, and re-layouts: 0.03 us -> 10.4 us  [shards(): jnp.concatenate([shift(pool_col, t - 2) for t in range(taps)], axis=1)]
    all_to_all x1, blocking collectives: 32 us -> 22.9 us  [to_rows(): got = lax.all_to_all(blocks, 'seq', 0, 0, tiled=True)]
    dot_general x2 -> x0, matrix products: 7.25 us -> none  [the longest x1 3.74 us: shards(): jnp.dot(cot_taps, dec_mat, preferred_element_type=F32).astype(BF16)]
  transfers between devices with their start and end apart: 3 -> 3, of which waited for: 2 -> 2; matrix products, arithmetic and copies ran while one was open for 3% -> 6% of each run, Pallas kernels for 0% -> 0%
where the time goes in v2:
time: 276 us; the launch traced here: 275 us
  Pallas kernels  124 us (45%)
  blocking collectives  49.2 us (18%)
  local copies, waits for them, and re-layouts  42.6 us (15%)
  waiting for transfers between devices  16.5 us (6%)
  matrix products  14.6 us (5%)
  between operations  14 us (5%)
  other arithmetic  13 us (5%)
    pallas_call x1, Pallas kernels, ring(): pl.pallas_call(functools.partial(ring_kernel, n), out_shape=jax.ShapeDtyp...  124 us
    all_to_all x1, blocking collectives, to_columns(): return lax.all_to_all(blocks, 'seq', 0, 0, tiled=True)  23.9 us
    all_to_all x1, blocking collectives, to_rows(): got = lax.all_to_all(blocks, 'seq', 0, 0, tiled=True)  22.9 us
    concatenate x2, local copies, waits for them, and re-layouts, shards(): jnp.concatenate([shift(pool_col, t - 2) for t in range(taps)], axis=1)  10.4 us
    reduce_scatter x1, waiting for transfers between devices, shards(): mine = lax.psum_scatter(mine, 'chan', scatter_dimension=1, tiled=True)  8.92 us
    all_gather x1, waiting for transfers between devices, shards(): columns = lax.all_gather(columns, 'chan', axis=1, tiled=True)  7.55 us
  transfers between devices with their start and end apart: 3, of which 2 were waited for; matrix products, arithmetic and copies ran while one was open for 6% of the time, Pallas kernels for 0%

profile of v2, /device:TPU:0, one launch (start us, length us, event | category | flops | bytes accessed | tf_op | source)
XLA Modules:
  0.0 274.6 jit_solution(11600430113892297644)
XLA Ops:
  7.2 2.2 reshape.92
  9.4 1.9 reduce_sum.9
  11.7 2.4 all_gather.9
  14.3 23.9 %all_to_all.10 = bf16[8,384,96]{1,2,0:T(8,128)(2,1)} all-to-all(bf16[8,384,96]{1,2,0:T(8,128)(2,1)S(1)} %bitcast.77), channel_id=1, replica_groups=mesh['groups'=2,'seq'=8,'chan'=2] {'seq'}, dimensions={0} | all-to-all | bytes 1179648 | tf_op jit(solution)/shard_map/all_to_all | solution.py:28
  38.5 7.5 %all-gather.6.cloned.1.call-done = bf16[8,768,96]{1,2,0:T(8,128)(2,1)} async-done(((bf16[8,384,96]{1,2,0:T(8,128)(2,1)}), bf16[8,768,96]{1,2,0:T(8,128)(2,1)}) %all-gather.6.cloned.1.call-update) | async-done | bytes 1179664 | tf_op jit(solution)/shard_map/all_gather | solution.py:245
  46.0 1.8 copy.49
  48.4 1.5 fusion.30
  50.7 1.0 concatenate.74
  51.7 1.0 concatenate.76
  55.9 1.0 concatenate.87
  57.8 4.4 %concatenate.88 = bf16[2048,480]{1,0:T(8,128)(2,1)S(1)} concatenate(bf16[2048,96]{1,0:T(8,128)(2,1)} %concatenate.84, bf16[2048,96]{1,0:T(8,128)(2,1)} %copy-done.5, bf16[2048,96]{1,0:T(8,128)(2,1)S(1)} %get-tuple-element.27, bf16[2048,96]{1,0:T(8,128)(2,1)} %pad_maximum_fusion.3, bf16[2048,96]{1,0:T(8,128)(2,1)} %concatenate.87), dimensions={1} | concatenate | bytes 3932160 | tf_op jit(solution)/shard_map/concatenate | solution.py:254
  62.2 5.2 %concatenate.83.x_ref = bf16[8,256,480]{2,1,0:T(8,128)(2,1)} concatenate(bf16[8,256,96]{2,1,0:T(8,128)(2,1)} %bitcast.67, bf16[8,256,96]{2,1,0:T(8,128)(2,1)} %bitcast.68, bf16[8,256,96]{2,1,0:T(8,128)(2,1)S(1)} %bitcast.56, bf16[8,256,96]{2,1,0:T(8,128)(2,1)} %bitcast.69, bf16[8,256,96]{2,1,0:T(8,128)(2,1)} %bitcast.70), dimensions={2} | concatenate | bytes 3932160 | tf_op jit(solution)/shard_map/concatenate | solution.py:253
  67.4 1.6 copy-done
  69.0 1.1 copy-done.2
  70.1 124.0 %shard_map.75 = bf16[8,256,1536]{2,1,0:T(8,128)(2,1)} custom-call(bf16[8,256,480]{2,1,0:T(8,128)(2,1)S(1)} %copy-done, bf16[8,256,480]{2,1,0:T(8,128)(2,1)S(1)} %bitcast.49, bf16[480,768]{1,0:T(8,128)(2,1)S(1)} %bitcast.52, bf16[480,768]{1,0:T(8,128)(2,1)S(1)} %bitcast.50), custom_call_target="tpu_custom_call" | custom-call | flops 3019898880 | bytes 12582912 | tf_op jit(solution)/shard_map/pallas_call | solution.py:198
  194.1 3.8 %fusion.6 = f32[2048,480]{0,1:T(8,128)S(1)} fusion(bf16[480,768]{1,0:T(8,128)(2,1)S(1)} %bitcast.51, bf16[2048,1536]{1,0:T(8,128)(2,1)} %bitcast.61), kind=kOutput, calls=%fused_computation.6 | convolution fusion | flops 1509949440 | bytes 7815168 | tf_op jit(solution)/shard_map/dot_general | solution.py:275
  197.9 1.7 fusion.2
  199.6 1.7 fusion.28
  201.3 1.4 fusion.29
  203.9 2.0 copy.42
  205.9 2.6 fusion.17
  208.7 2.7 pad_maximum_fusion
  211.7 8.9 %reduce-scatter.2.cloned.1.call-done = bf16[8,384,96]{2,1,0:T(8,128)(2,1)} async-done(((bf16[8,768,96]{2,1,0:T(8,128)(2,1)}), bf16[8,384,96]{2,1,0:T(8,128)(2,1)}) %reduce-scatter.2.cloned.1.call-update) | async-done | bytes 589840 | tf_op jit(solution)/shard_map/reduce_scatter | solution.py:286
  220.6 2.2 copy.44
  222.8 22.9 %all_to_all.11 = bf16[8,384,96]{1,2,0:T(8,128)(2,1)} all-to-all(bf16[8,384,96]{1,2,0:T(8,128)(2,1)} %copy.44), channel_id=1, replica_groups=mesh['groups'=2,'seq'=8,'chan'=2] {'seq'}, dimensions={0} | all-to-all | bytes 1179648 | tf_op jit(solution)/shard_map/all_to_all | solution.py:33
  245.7 1.0 constant_dynamic-slice_fusion.1
  247.7 5.2 %concatenate.98 = bf16[2048,480]{1,0:T(8,128)(2,1)} concatenate(bf16[2048,96]{1,0:T(8,128)(2,1)S(1)} %copy-done.4, bf16[2048,96]{1,0:T(8,128)(2,1)} %concatenate.76, bf16[2048,96]{1,0:T(8,128)(2,1)S(1)} %bitcast.57, bf16[2048,96]{1,0:T(8,128)(2,1)} %concatenate.79, bf16[2048,96]{1,0:T(8,128)(2,1)} %concatenate.81), dimensions={1} | concatenate | bytes 3932160 | tf_op jit(solution)/shard_map/concatenate | solution.py:253
  252.9 4.6 %fusion.8 = bf16[480,768]{1,0:T(8,128)(2,1)} fusion(bf16[2048,480]{1,0:T(8,128)(2,1)S(1)} %concatenate.88, bf16[2048,1536]{1,0:T(8,128)(2,1)} %bitcast.62), kind=kOutput, calls=%fused_computation.9 | convolution fusion | flops 1510318080 | bytes 5849088 | tf_op jit(solution)/shard_map/dot_general | solution.py:270
  257.5 4.5 %fusion.11 = bf16[480,768]{1,0:T(8,128)(2,1)} fusion(bf16[2048,480]{1,0:T(8,128)(2,1)S(1)} %copy-done.7, bf16[2048,1536]{1,0:T(8,128)(2,1)} %bitcast.63), kind=kOutput, calls=%fused_computation.10 | convolution fusion | flops 1510318080 | bytes 5849088 | tf_op jit(solution)/shard_map/dot_general | solution.py:271
  262.0 1.1 dynamic-slice_convert_fusion
  264.2 1.8 add_convert_fusion.2
  266.0 1.1 fusion.14
  (51 shorter events, 10.8 us)
Async XLA Ops:
  7.2 4.3 %copy-start.8 = (bf16[512,384]{1,0:T(8,128)(2,1)S(1)}, bf16[512,384]{1,0:T(8,128)(2,1)}, u32[]{:S(2)}) copy-start(bf16[512,384]{1,0:T(8,128)(2,1)} %param.7) | copy-start | bytes 1179652
  7.2 38.8 %all-gather.6.cloned.1.call-start = ((), (), s32[]{:S(2)}) async-start(), calls=%async_computation.5 | async-start | bytes 1769472 | tf_op jit(solution)/shard_map/all_gather | solution.py:245
  38.2 182.4 %reduce-scatter.2.cloned.1.call-start = ((), (), s32[]{:S(2)}) async-start(), calls=%async_computation.3 | async-start | bytes 2359296 | tf_op jit(solution)/shard_map/reduce_scatter | solution.py:286
  54.8 2.1 copy-start.5
  62.2 5.2 %copy-start.1 = (bf16[96,5,768]{2,0,1:T(8,128)(2,1)S(1)}, bf16[96,5,768]{2,0,1:T(8,128)(2,1)}, u32[]{:S(2)}) copy-start(bf16[96,5,768]{2,0,1:T(8,128)(2,1)} %param.6) | copy-start | bytes 2211844
  67.4 1.6 copy-start
  69.0 1.1 copy-start.2
  194.1 3.8 %copy-start.3 = (bf16[8,256,1536]{2,1,0:T(8,128)(2,1)S(1)}, bf16[8,256,1536]{2,1,0:T(8,128)(2,1)}, u32[]{:S(2)}) copy-start(bf16[8,256,1536]{2,1,0:T(8,128)(2,1)} %shard_map.75) | copy-start | bytes 18874372
  199.6 3.1 %copy-start.6 = (f32[2048,480]{0,1:T(8,128)}, f32[2048,480]{0,1:T(8,128)S(1)}, u32[]{:S(2)}) copy-start(f32[2048,480]{0,1:T(8,128)S(1)} %fusion.2) | copy-start | bytes 11796484
  211.4 36.3 %copy-start.4 = (bf16[2048,96]{1,0:T(8,128)(2,1)S(1)}, bf16[2048,96]{1,0:T(8,128)(2,1)}, u32[]{:S(2)}) copy-start(bf16[2048,96]{1,0:T(8,128)(2,1)} %concatenate.74) | copy-start | bytes 1179652
  211.4 50.6 %all-gather.4.cloned.1.call-start = ((), (), s32[]{:S(2)}) async-start(), calls=%async_computation.4 | async-start | bytes 1769472 | tf_op jit(solution)/shard_map/all_gather | solution.py:287
  252.9 4.6 %copy-start.7 = (bf16[2048,480]{1,0:T(8,128)(2,1)S(1)}, bf16[2048,480]{1,0:T(8,128)(2,1)}, u32[]{:S(2)}) copy-start(bf16[2048,480]{1,0:T(8,128)(2,1)} %concatenate.98) | copy-start | bytes 5898244
Sparse Core Ops, SparseCore 0:
  38.4 7.6 all-gather.5
  211.5 9.0 reduce-scatter.1
  245.8 7.5 all-gather.3

commit v3 on v2

--- a/solution.py
+++ b/solution.py
@@ -221,7 +221,7 @@
     )(pool_taps, cot_taps, enc_mat, dec_mat)
 
 
-def shards(inputs, enc_weight, dec_weight, cotangent):
+def wide_shards(inputs, enc_weight, dec_weight, cotangent):
     parts = lax.axis_size("seq")
     rows, width = inputs.shape
     half = rows // 2
@@ -294,6 +294,328 @@
     return mixed_out, input_grad, enc_grad, dec_grad
 
 
+PAD = 8
+LANES = 128
+
+
+def whole_kernel(
+    n, own_ref, enc_ref, dec_ref, enc_grad_ref, dec_grad_ref, out_ref, gathered,
+    both, padded, x_ref, y_ref, slots, term, mine, stage, acc, leaving, arriving,
+    enc_sum, dec_sum, rs_send, rs_recv, ag_send, ag_recv, local_sem, stage_sem, pair_send, pair_recv,
+):
+    me = lax.axis_index("seq")
+    core = lax.axis_index("chan")
+    place = ring_place(me, n)
+    nexts = (ring_index(place + 1, n), ring_index(place - 1, n))
+    few, block = own_ref.shape[2:]
+    half = 2 * few
+    total = n * half
+    share = enc_ref.shape[1]
+    side = half // 2
+    piece = side // PIECES
+    mesh_ids = pl.DeviceIdType.MESH
+
+    barrier = pltpu.get_barrier_semaphore()
+    for other in nexts:
+        pl.semaphore_signal(barrier, inc=1, device_id={"seq": other}, device_id_type=mesh_ids)
+    pl.semaphore_signal(barrier, inc=1, device_id={"chan": 1 - core}, device_id_type=mesh_ids)
+    pl.semaphore_wait(barrier, 3)
+
+    def pair_copy(k, src, dst):
+        return pltpu.make_async_remote_copy(
+            src_ref=src,
+            dst_ref=dst,
+            send_sem=pair_send.at[k],
+            recv_sem=pair_recv.at[k],
+            device_id={"chan": 1 - core},
+            device_id_type=mesh_ids,
+        )
+
+    swap = pair_copy(0, own_ref, both.at[core])
+    swap.start()
+    keep = pltpu.make_async_copy(own_ref, both.at[core], local_sem)
+    keep.start()
+    padded[...] = jnp.zeros_like(padded)
+    x_ref[...] = jnp.zeros_like(x_ref)
+    y_ref[...] = jnp.zeros_like(y_ref)
+    acc[...] = jnp.zeros_like(acc)
+    enc_sum[...] = jnp.zeros_like(enc_sum)
+    dec_sum[...] = jnp.zeros_like(dec_sum)
+    keep.wait()
+    swap.wait()
+
+    def widen(chunk, carry):
+        for part in range(2):
+            for k in range(3):
+                at = pl.ds(pl.multiple_of(PAD + chunk * half + part * few, 8), few)
+                padded[k, at, :block] = both[part, k, chunk].astype(F32)
+        return carry
+
+    lax.fori_loop(0, n, widen, 0)
+
+    def taps_of(chunk, carry):
+        def rows(k, by):
+            return padded[k, pl.ds(chunk * half + (PAD + by), half), :block]
+
+        for t in range(5):
+            x_ref[chunk, :, t * LANES : t * LANES + block] = rows(0, t - 2).astype(BF16)
+        for t, (a, b) in enumerate(((1, 1), (1, 0), (0, 0), (0, -1), (-1, -1))):
+            both_rows = rows(1, a) + rows(2, b)
+            y_ref[chunk, :, t * LANES : t * LANES + block] = both_rows.astype(BF16)
+        return carry
+
+    lax.fori_loop(0, n, taps_of, 0)
+
+    def signed(d, steps):
+        return place - steps if d == 0 else place + steps
+
+    def own_term(d, steps):
+        chunk = ring_index(signed(d, steps), n)
+        at = pl.ds(d * side, side)
+        a = jnp.dot(x_ref[chunk, at, :], enc_ref[...], preferred_element_type=F32)
+        b = jnp.dot(y_ref[chunk, at, :], dec_ref[...], preferred_element_type=F32)
+        return a, b
+
+    def rs_copy(d, s, q):
+        at = pl.ds(q * piece, piece)
+        return pltpu.make_async_remote_copy(
+            src_ref=slots.at[d, s, at],
+            dst_ref=slots.at[d, s + 1, at],
+            send_sem=rs_send.at[d, s, q],
+            recv_sem=rs_recv.at[d, s, q],
+            device_id={"seq": nexts[d]},
+            device_id_type=mesh_ids,
+        )
+
+    def ag_copy(d, s, q, first, owner_steps):
+        at = pl.ds(d * side + q * piece, piece)
+        owner = ring_index(signed(d, owner_steps), n)
+        return pltpu.make_async_remote_copy(
+            src_ref=mine.at[at] if first else gathered.at[owner, at],
+            dst_ref=gathered.at[owner, at],
+            send_sem=ag_send.at[d, s, q],
+            recv_sem=ag_recv.at[d, s, q],
+            device_id={"seq": nexts[d]},
+            device_id_type=mesh_ids,
+        )
+
+    for d in range(2):
+        a, b = own_term(d, 1)
+        slots[d, 0, :, :share] = a.astype(BF16)
+        slots[d, 0, :, share:] = b.astype(BF16)
+        for q in range(PIECES):
+            rs_copy(d, 0, q).start()
+
+    def fill(s):
+        for d in range(2):
+            a, b = own_term(d, s + 2)
+            term[d, :, :share] = a
+            term[d, :, share:] = b
+
+    def rs_step(s, carry):
+        fill(s)
+        for q in range(PIECES):
+            at = pl.ds(q * piece, piece)
+            for d in range(2):
+                rs_copy(d, s, q).wait_recv()
+                summed = slots[d, s + 1, at, :].astype(F32) + term[d, at, :]
+                slots[d, s + 1, at, :] = summed.astype(BF16)
+                rs_copy(d, s + 1, q).start()
+        return carry
+
+    lax.fori_loop(0, n - 2, rs_step, 0)
+    fill(n - 2)
+    for q in range(PIECES):
+        at = pl.ds(q * piece, piece)
+        for d in range(2):
+            rs_copy(d, n - 2, q).wait_recv()
+            rows = pl.ds(d * side + q * piece, piece)
+            pre = slots[d, n - 1, at, :share].astype(F32) + term[d, at, :share]
+            grad = slots[d, n - 1, at, share:].astype(F32) + term[d, at, share:]
+            value, slope = gelu_and_slope(pre)
+            mine[rows, :share] = value.astype(BF16)
+            mine[rows, share:] = (grad * slope).astype(BF16)
+            ag_copy(d, 0, q, True, 0).start()
+
+    contract_rows = (((0,), (0,)), ((), ()))
+    contract_last = (((1,), (1,)), ((), ()))
+
+    def consume(chunk, d, load):
+        at = pl.ds(d * side, side)
+        hid = load(slice(None, share))
+        pre_grad = load(slice(share, None))
+        dec_sum[...] += lax.dot_general(
+            y_ref[chunk, at, :], hid, contract_rows, preferred_element_type=F32
+        )
+        enc_sum[...] += lax.dot_general(
+            x_ref[chunk, at, :], pre_grad, contract_rows, preferred_element_type=F32
+        )
+        p = lax.dot_general(hid, dec_ref[...], contract_last, preferred_element_type=F32)
+        g = lax.dot_general(pre_grad, enc_ref[...], contract_last, preferred_element_type=F32)
+        p = [p[:, t * LANES : (t + 1) * LANES] for t in range(5)]
+        base = chunk * half + (PAD + d * side)
+
+        def add(k, by, what):
+            to = pl.ds(base + by, side)
+            acc[k, to, :] += what
+
+        add(1, 1, p[0] + p[1])
+        add(1, 0, p[2] + p[3])
+        add(1, -1, p[4])
+        add(2, 1, p[0])
+        add(2, 0, p[1] + p[2])
+        add(2, -1, p[3] + p[4])
+        for t in range(5):
+            add(0, t - 2, g[:, t * LANES : (t + 1) * LANES])
+
+    for d in range(2):
+        consume(me, d, lambda cols: mine[d * side : (d + 1) * side, cols])
+
+    def stage_copy(d, s):
+        owner = ring_index(signed(d, s + 1), n)
+        return pltpu.make_async_copy(
+            gathered.at[owner, pl.ds(d * side, side)], stage.at[d], stage_sem.at[d]
+        )
+
+    def take(s):
+        for d in range(2):
+            stage_copy(d, s).start()
+        for d in range(2):
+            stage_copy(d, s).wait()
+            consume(ring_index(signed(d, s + 1), n), d, lambda cols: stage[d, :, cols])
+
+    def ag_step(s, carry):
+        for q in range(PIECES):
+            for d in range(2):
+                ag_copy(d, s, q, True, s + 1).wait_recv()
+                ag_copy(d, s + 1, q, False, s + 1).start()
+        take(s)
+        return carry
+
+    lax.fori_loop(0, n - 2, ag_step, 0)
+    for q in range(PIECES):
+        for d in range(2):
+            ag_copy(d, n - 2, q, True, n - 1).wait_recv()
+    take(n - 2)
+
+    def pick(k, chunk, part):
+        at = pl.ds(pl.multiple_of(PAD + chunk * half + part * few, 8), few)
+        return acc[k, at, :block]
+
+    def pack(chunk, carry):
+        for k in range(3):
+            leaving[k, chunk] = pick(k, chunk, 1 - core).astype(BF16)
+        return carry
+
+    lax.fori_loop(0, n, pack, 0)
+    swap2 = pair_copy(1, leaving, arriving)
+    swap2.start()
+    enc_grad_ref[...] = enc_sum[...].astype(BF16)
+    dec_grad_ref[...] = dec_sum[...].astype(BF16)
+
+    def drain(s, carry):
+        for q in range(PIECES):
+            for d in range(2):
+                rs_copy(d, s, q).wait_send()
+                ag_copy(d, s, q, True, s).wait_send()
+        return carry
+
+    lax.fori_loop(0, n - 1, drain, 0)
+    swap2.wait()
+
+    def finish(chunk, carry):
+        for k in range(3):
+            summed = pick(k, chunk, core) + arriving[k, chunk].astype(F32)
+            out_ref[chunk, k * few : (k + 1) * few, :] = summed.astype(BF16)
+        return carry
+
+    lax.fori_loop(0, n, finish, 0)
+
+
+def whole_ring(own, enc_mat, dec_mat):
+    n, few, block = own.shape[1:]
+    half = 2 * few
+    depth, share = enc_mat.shape
+    vmem = pl.BlockSpec(memory_space=pltpu.VMEM)
+    steps = (2, n - 1, PIECES)
+    dma = pltpu.SemaphoreType.DMA
+    return pl.pallas_call(
+        functools.partial(whole_kernel, n),
+        out_shape=[
+            jax.ShapeDtypeStruct((depth, share), BF16),
+            jax.ShapeDtypeStruct((depth, share), BF16),
+            jax.ShapeDtypeStruct((n, 3 * few, block), BF16),
+            jax.ShapeDtypeStruct((n, half, 2 * share), BF16),
+        ],
+        in_specs=[vmem] * 3,
+        out_specs=[vmem] * 3 + [pl.BlockSpec(memory_space=pl.ANY)],
+        scratch_shapes=[
+            pltpu.VMEM((2,) + own.shape, BF16),
+            pltpu.VMEM((3, n * half + 2 * PAD, LANES), F32),
+            pltpu.VMEM((n, half, depth), BF16),
+            pltpu.VMEM((n, half, depth), BF16),
+            pltpu.VMEM((2, n, half // 2, 2 * share), BF16),
+            pltpu.VMEM((2, half // 2, 2 * share), F32),
+            pltpu.VMEM((half, 2 * share), BF16),
+            pltpu.VMEM((2, half // 2, 2 * share), BF16),
+            pltpu.VMEM((3, n * half + 2 * PAD, LANES), F32),
+            pltpu.VMEM(own.shape, BF16),
+            pltpu.VMEM(own.shape, BF16),
+            pltpu.VMEM((depth, share), F32),
+            pltpu.VMEM((depth, share), F32),
+            dma(steps), dma(steps), dma(steps), dma(steps), dma, dma((2,)), dma((2,)), dma((2,)),
+        ],
+        compiler_params=pltpu.CompilerParams(
+            collective_id=0, has_side_effects=True, vmem_limit_bytes=56 * 2**20
+        ),
+        cost_estimate=pl.CostEstimate(
+            flops=12 * n * half * depth * share,
+            bytes_accessed=8 * n * half * share,
+            transcendentals=half * share,
+        ),
+    )(own, enc_mat, dec_mat)[:3]
+
+
+def shards(inputs, enc_weight, dec_weight, cotangent):
+    parts = lax.axis_size("seq")
+    cores = lax.axis_size("chan")
+    rows, width = inputs.shape
+    half = rows // 2
+    few = half // 2
+    block, taps, share = enc_weight.shape
+    half_width = cotangent.shape[1]
+    if cores != 2 or taps != 5 or block > LANES or parts * half > 2048:
+        return wide_shards(inputs, enc_weight, dec_weight, cotangent)
+    core = lax.axis_index("chan")
+
+    some = lax.dynamic_slice_in_dim(inputs, core * half, half, 0)
+    pooled = (some.astype(F32).reshape(few, 2, width).sum(axis=1) * 0.5).astype(BF16)
+    cot_full = lax.all_gather(cotangent, "chan", axis=1, tiled=True)
+    cot_some = lax.dynamic_slice_in_dim(cot_full, core * half, half, 0).reshape(few, 2, width)
+    leaving = jnp.concatenate([pooled, cot_some[:, 0], cot_some[:, 1]], axis=0)
+    columns = to_columns(leaving, parts).reshape(parts, 3, few, block).transpose(1, 0, 2, 3)
+
+    def matrix(weight):
+        fill = ((0, 0), (0, LANES - block), (0, 0))
+        return jnp.pad(weight.transpose(1, 0, 2), fill).reshape(taps * LANES, share)
+
+    enc_grad, dec_grad, back = whole_ring(columns, matrix(enc_weight), matrix(dec_weight))
+
+    def unfold(grad):
+        return grad.reshape(taps, LANES, share)[:, :block].transpose(1, 0, 2)
+
+    mine = lax.all_gather(to_rows(back), "chan", axis=0, tiled=False)
+    col_start = core * half_width
+    mine = lax.dynamic_slice_in_dim(mine, col_start, half_width, 2).astype(F32)
+    mine = mine.reshape(2, 3, few, half_width)
+    pool_grad = mine[:, 0].reshape(half, half_width)
+    decoded = jnp.stack([mine[:, 1], mine[:, 2]], axis=2).reshape(rows, half_width)
+    skip = lax.dynamic_slice_in_dim(inputs, col_start, half_width, 1)
+    mixed_out = (skip.astype(F32) + decoded).astype(BF16)
+    input_grad = (cotangent.astype(F32) + 0.5 * jnp.repeat(pool_grad, 2, axis=0)).astype(BF16)
+    return mixed_out, input_grad, unfold(enc_grad), unfold(dec_grad)
+
+
 def solution(mesh):
     return jax.shard_map(
         shards,

time: 276 us -> 218 us (0.79)
  local copies, waits for them, and re-layouts: 42.6 us -> 13.8 us
  blocking collectives: 49.2 us -> 23.3 us
  matrix products: 14.6 us -> 0 us
  Pallas kernels: 124 us -> 135 us
  other arithmetic: 13 us -> 3.78 us
  starting transfers between devices: 0.52 us -> 7.55 us
  waiting for transfers between devices: 16.5 us -> 19.4 us
    all_to_all x1 -> x0, blocking collectives: 23.9 us -> none  [to_columns(): return lax.all_to_all(blocks, 'seq', 0, 0, tiled=True)]
    concatenate x9 -> x0, local copies, waits for them, and re-layouts: 20.4 us -> none  [the longest x2 10.4 us: shards(): jnp.concatenate([shift(pool_col, t - 2) for t in range(taps)], axis=1)]
    dot_general x4 -> x0, matrix products: 14.6 us -> none  [the longest x1 4.64 us: shards(): lax.dot_general(cot_taps, hidden_all, contract_rows, preferred_element_ty...]
    all_to_all x0 -> x1, waiting for transfers between devices: none -> 13.8 us  [to_columns(): return lax.all_to_all(blocks, 'seq', 0, 0, tiled=True)]
    pallas_call x1, Pallas kernels: 124 us -> 135 us  [whole_ring(): pl.pallas_call(functools.partial(whole_kernel, n), out_shape=[jax.ShapeDt...]
    reduce_scatter x1 -> x0, waiting for transfers between devices: 8.92 us -> none  [shards(): mine = lax.psum_scatter(mine, 'chan', scatter_dimension=1, tiled=True)]
    all_to_all x0 -> x1, starting transfers between devices: none -> 7.33 us  [to_columns(): return lax.all_to_all(blocks, 'seq', 0, 0, tiled=True)]
    slice x11 -> x3, local copies, waits for them, and re-layouts: 6.68 us -> 1.36 us  [shards(): leaving = jnp.concatenate([pooled, cot_some[:, 0], cot_some[:, 1]], axis=0)]
  transfers between devices with their start and end apart: 3 -> 2, of which waited for: 2 -> 2; matrix products, arithmetic and copies ran while one was open for 6% -> 2% of each run, Pallas kernels for 0% -> 0%
where the time goes in v3:
time: 218 us
  Pallas kernels  135 us (62%)
  blocking collectives  23.3 us (11%)
  waiting for transfers between devices  19.4 us (9%)
  between operations  14.2 us (7%)
  local copies, waits for them, and re-layouts  13.8 us (6%)
  starting transfers between devices  7.55 us (3%)
  other arithmetic  3.78 us (2%)
    pallas_call x1, Pallas kernels, whole_ring(): pl.pallas_call(functools.partial(whole_kernel, n), out_shape=[jax.ShapeDt...  135 us
    all_to_all x1, blocking collectives, to_rows(): got = lax.all_to_all(blocks, 'seq', 0, 0, tiled=True)  20.5 us
    all_to_all x1, waiting for transfers between devices, to_columns(): return lax.all_to_all(blocks, 'seq', 0, 0, tiled=True)  13.8 us
    all_to_all x1, starting transfers between devices, to_columns(): return lax.all_to_all(blocks, 'seq', 0, 0, tiled=True)  7.33 us
    all_gather x1, waiting for transfers between devices, shards(): mine = lax.all_gather(to_rows(back), 'chan', axis=0, tiled=False)  5.51 us
  transfers between devices with their start and end apart: 2, of which 2 were waited for; matrix products, arithmetic and copies ran while one was open for 2% of the time, Pallas kernels for 0%

profile of v3, /device:TPU:0, one launch (start us, length us, event | category | flops | bytes accessed | tf_op | source)
XLA Modules:
  0.0 217.5 jit_solution(13533912668555318225)
XLA Ops:
  7.2 2.8 %all_gather.6 = bf16[512,768]{1,0:T(8,128)(2,1)S(1)} all-gather(bf16[512,384]{1,0:T(8,128)(2,1)} %param.7), channel_id=1, replica_groups=mesh['groups'=2,'seq'=8,'chan'=2] {'chan'}, dimensions={1}, use_global_device_ids=true | all-gather | bytes 1179648 | tf_op jit(solution)/shard_map/all_gather | solution.py:593
  10.1 0.5 reshape.68
  10.5 0.9 reduce_sum.9
  11.5 0.2 copy.19
  11.7 0.1 reshape.58
  11.8 0.5 fusion
  12.4 0.4 copy.20
  12.8 0.4 copy.21
  13.2 0.9 maximum_bitcast_fusion
  14.1 7.3 %all-to-all-start = ((bf16[8,384,96]{1,2,0:T(8,128)(2,1)}), bf16[8,384,96]{1,2,0:T(8,128)(2,1)S(1)}, u32[]{:S(2)}, u32[]{:S(2)}) async-start(bf16[8,384,96]{1,2,0:T(8,128)(2,1)} %maximum_bitcast_fusion), calls=%async_computation | async-start | bytes 1179648 | tf_op jit(solution)/shard_map/all_to_all | solution.py:28
  21.4 0.2 all-gather.2.cloned.1.call-start
  21.7 1.1 pad.7
  22.8 1.0 pad.8
  23.8 13.8 %all-to-all-done = bf16[8,384,96]{1,2,0:T(8,128)(2,1)S(1)} async-done(((bf16[8,384,96]{1,2,0:T(8,128)(2,1)}), bf16[8,384,96]{1,2,0:T(8,128)(2,1)S(1)}, u32[]{:S(2)}, u32[]{:S(2)}) %all-to-all-start) | async-done | bytes 589856 | tf_op jit(solution)/shard_map/all_to_all | solution.py:28
  37.6 0.2 reshape.59
  37.8 1.3 copy.22
  39.2 135.4 %shard_map.75 = (bf16[640,768]{1,0:T(8,128)(2,1)}, bf16[640,768]{1,0:T(8,128)(2,1)}, bf16[8,384,96]{2,1,0:T(8,128)(2,1)}, bf16[8,256,1536]{2,1,0:T(8,128)(2,1)}) custom-call(bf16[3,8,128,96]{3,2,1,0:T(8,128)(2,1)} %bitcast.36, bf16[640,768]{1,0:T(8,128)(2,1)} %bitcast.33, bf16[640,768]{1,0:T(8,128)(2,1)} %bitcast.34), custom_call_target="tpu_custom_call" | custom-call | flops 12079595520 | bytes 12582912 | tf_op jit(solution)/shard_map/pallas_call | solution.py:542
  174.6 1.5 copy.23
  176.1 20.5 %all_to_all.10 = bf16[8,384,96]{1,2,0:T(8,128)(2,1)S(1)} all-to-all(bf16[8,384,96]{1,2,0:T(8,128)(2,1)S(1)} %copy.23), channel_id=1, replica_groups=mesh['groups'=2,'seq'=8,'chan'=2] {'seq'}, dimensions={0} | all-to-all | bytes 1179648 | tf_op jit(solution)/shard_map/all_to_all | solution.py:33
  196.6 1.1 copy.24
  197.8 0.9 slice_bitcast_fusion.1
  198.7 0.3 copy-done.4
  199.1 0.9 slice_bitcast_fusion
  200.0 5.5 %all-gather.2.cloned.1.call-done = bf16[2,384,768]{2,1,0:T(8,128)(2,1)} async-done(((bf16[1,384,768]{2,1,0:T(8,128)(2,1)}), bf16[2,384,768]{2,1,0:T(8,128)(2,1)}) %all-gather.2.cloned.1.call-update) | async-done | bytes 1179664 | tf_op jit(solution)/shard_map/all_gather | solution.py:607
  205.5 1.1 constant_dynamic-slice_fusion
  206.8 0.3 broadcast_in_dim.3
  207.1 0.5 mul.35
  207.6 0.2 copy-done
  207.8 0.8 add_convert_fusion
  208.7 0.6 copy.26
  209.3 0.5 reshape.64
  209.8 0.8 add_convert_fusion.1
  (16 shorter events, 0.5 us)
Async XLA Ops:
  7.2 2.8 %copy-start.1 = (bf16[512,768]{1,0:T(8,128)(2,1)S(1)}, bf16[512,768]{1,0:T(8,128)(2,1)}, u32[]{:S(2)}) copy-start(bf16[512,768]{1,0:T(8,128)(2,1)} %param.4) | copy-start | bytes 2359300
  13.2 8.5 %copy-start.2 = (bf16[96,5,768]{2,0,1:T(8,128)(2,1)S(1)}, bf16[96,5,768]{2,0,1:T(8,128)(2,1)}, u32[]{:S(2)}) copy-start(bf16[96,5,768]{2,0,1:T(8,128)(2,1)} %param.5) | copy-start | bytes 2211844
  14.1 8.7 %copy-start.3 = (bf16[96,5,768]{2,0,1:T(8,128)(2,1)S(1)}, bf16[96,5,768]{2,0,1:T(8,128)(2,1)}, u32[]{:S(2)}) copy-start(bf16[96,5,768]{2,0,1:T(8,128)(2,1)} %param.6) | copy-start | bytes 2211844
  14.1 23.5 %all-to-all-start = ((bf16[8,384,96]{1,2,0:T(8,128)(2,1)}), bf16[8,384,96]{1,2,0:T(8,128)(2,1)S(1)}, u32[]{:S(2)}, u32[]{:S(2)}) async-start(bf16[8,384,96]{1,2,0:T(8,128)(2,1)} %maximum_bitcast_fusion), calls=%async_computation | async-start | bytes 1179648 | tf_op jit(solution)/shard_map/all_to_all | solution.py:28
  21.4 184.0 %all-gather.2.cloned.1.call-start = ((), (), s32[]{:S(2)}) async-start(), calls=%async_computation.2 | async-start | bytes 1769472 | tf_op jit(solution)/shard_map/all_gather | solution.py:607
  196.6 1.2 copy-start.5
  197.7 1.4 copy-start.4
  206.8 1.0 copy-start
Sparse Core Ops, SparseCore 0:
  197.8 7.6 all-gather.1

commit v4 on v3

--- a/solution.py
+++ b/solution.py
@@ -300,40 +300,54 @@
 
 def whole_kernel(
     n, own_ref, enc_ref, dec_ref, enc_grad_ref, dec_grad_ref, out_ref, gathered,
-    both, padded, x_ref, y_ref, slots, term, mine, stage, acc, leaving, arriving,
-    enc_sum, dec_sum, rs_send, rs_recv, ag_send, ag_recv, local_sem, stage_sem, pair_send, pair_recv,
+    both, padded, x_ref, y_ref, slots, term, mine, stage, acc, leaving, arriving, settled, landed,
+    enc_sum, dec_sum, rs_send, rs_recv, ag_send, ag_recv, local_sem, stage_sem,
+    out_send, out_recv, pair_send, pair_recv, back_send, back_recv, sum_send, sum_recv, last_send, last_recv,
 ):
     me = lax.axis_index("seq")
     core = lax.axis_index("chan")
     place = ring_place(me, n)
     nexts = (ring_index(place + 1, n), ring_index(place - 1, n))
-    few, block = own_ref.shape[2:]
+    few, block = own_ref.shape[1] // 3, own_ref.shape[2]
     half = 2 * few
-    total = n * half
     share = enc_ref.shape[1]
     side = half // 2
     piece = side // PIECES
     mesh_ids = pl.DeviceIdType.MESH
 
     barrier = pltpu.get_barrier_semaphore()
-    for other in nexts:
+    around = [i if up else -i for i in range(1, n // 2 + 1) for up in (True, False)][: n - 1]
+    others = [ring_index(place + i, n) for i in around]
+    sources = [ring_index(place - i, n) for i in around]
+    for other in others:
         pl.semaphore_signal(barrier, inc=1, device_id={"seq": other}, device_id_type=mesh_ids)
     pl.semaphore_signal(barrier, inc=1, device_id={"chan": 1 - core}, device_id_type=mesh_ids)
-    pl.semaphore_wait(barrier, 3)
-
-    def pair_copy(k, src, dst):
+    pl.semaphore_wait(barrier, n)
+
+    def remote(src, dst, send, recv, where):
         return pltpu.make_async_remote_copy(
             src_ref=src,
             dst_ref=dst,
-            send_sem=pair_send.at[k],
-            recv_sem=pair_recv.at[k],
-            device_id={"chan": 1 - core},
+            send_sem=send,
+            recv_sem=recv,
+            device_id=where,
             device_id_type=mesh_ids,
         )
 
-    swap = pair_copy(0, own_ref, both.at[core])
-    swap.start()
-    keep = pltpu.make_async_copy(own_ref, both.at[core], local_sem)
+    other_core = {"chan": 1 - core}
+
+    def out_copy(i):
+        return remote(
+            own_ref.at[others[i]], both.at[core, me], out_send.at[i], out_recv.at[i], {"seq": others[i]}
+        )
+
+    def pair_copy(i, chunk, part):
+        block_of = both.at[part, chunk]
+        return remote(block_of, block_of, pair_send.at[i], pair_recv.at[i], other_core)
+
+    for i in range(n - 1):
+        out_copy(i).start()
+    keep = pltpu.make_async_copy(own_ref.at[me], both.at[core, me], local_sem)
     keep.start()
     padded[...] = jnp.zeros_like(padded)
     x_ref[...] = jnp.zeros_like(x_ref)
@@ -342,13 +356,21 @@
     enc_sum[...] = jnp.zeros_like(enc_sum)
     dec_sum[...] = jnp.zeros_like(dec_sum)
     keep.wait()
-    swap.wait()
+    pair_copy(n - 1, me, core).start()
+    for i in range(n - 1):
+        remote(
+            own_ref.at[me], both.at[core, sources[i]], out_send.at[i], out_recv.at[i], {"seq": others[i]}
+        ).wait_recv()
+        pair_copy(i, sources[i], core).start()
+    pair_copy(n - 1, me, 1 - core).wait_recv()
+    for i in range(n - 1):
+        pair_copy(i, sources[i], 1 - core).wait_recv()
 
     def widen(chunk, carry):
         for part in range(2):
             for k in range(3):
                 at = pl.ds(pl.multiple_of(PAD + chunk * half + part * few, 8), few)
-                padded[k, at, :block] = both[part, k, chunk].astype(F32)
+                padded[k, at, :block] = both[part, chunk, k * few : (k + 1) * few].astype(F32)
         return carry
 
     lax.fori_loop(0, n, widen, 0)
@@ -502,14 +524,28 @@
         at = pl.ds(pl.multiple_of(PAD + chunk * half + part * few, 8), few)
         return acc[k, at, :block]
 
-    def pack(chunk, carry):
+    def sum_copy(i, chunk):
+        return remote(leaving.at[chunk], arriving.at[chunk], sum_send.at[i], sum_recv.at[i], other_core)
+
+    def back_copy(i, to, at):
+        return remote(settled.at[to], landed.at[at], back_send.at[i], back_recv.at[i], {"seq": others[i]})
+
+    order = others + [me]
+    for i in range(n):
         for k in range(3):
-            leaving[k, chunk] = pick(k, chunk, 1 - core).astype(BF16)
-        return carry
-
-    lax.fori_loop(0, n, pack, 0)
-    swap2 = pair_copy(1, leaving, arriving)
-    swap2.start()
+            leaving[order[i], k * few : (k + 1) * few] = pick(k, order[i], 1 - core).astype(BF16)
+        sum_copy(i, order[i]).start()
+    for i in range(n):
+        chunk = order[i]
+        sum_copy(i, chunk).wait_recv()
+        for k in range(3):
+            at = slice(k * few, (k + 1) * few)
+            summed = pick(k, chunk, core) + arriving[chunk, at].astype(F32)
+            settled[chunk, at] = summed.astype(BF16)
+        if i < n - 1:
+            back_copy(i, chunk, me).start()
+    keep_back = pltpu.make_async_copy(settled.at[me], landed.at[me], local_sem)
+    keep_back.start()
     enc_grad_ref[...] = enc_sum[...].astype(BF16)
     dec_grad_ref[...] = dec_sum[...].astype(BF16)
 
@@ -521,20 +557,30 @@
         return carry
 
     lax.fori_loop(0, n - 1, drain, 0)
-    swap2.wait()
-
-    def finish(chunk, carry):
-        for k in range(3):
-            summed = pick(k, chunk, core) + arriving[k, chunk].astype(F32)
-            out_ref[chunk, k * few : (k + 1) * few, :] = summed.astype(BF16)
-        return carry
-
-    lax.fori_loop(0, n, finish, 0)
+    for i in range(n):
+        pair_copy(i, me, core).wait_send()
+        sum_copy(i, me).wait_send()
+    for i in range(n - 1):
+        out_copy(i).wait_send()
+    keep_back.wait()
+    for i in range(n - 1):
+        back_copy(i, me, sources[i]).wait_recv()
+    theirs = landed.at[pl.ds((1 - core) * (n // 2), n // 2)]
+    last = remote(theirs, out_ref.at[core], last_send, last_recv, other_core)
+    last.start()
+    ours = pltpu.make_async_copy(
+        landed.at[pl.ds(core * (n // 2), n // 2)], out_ref.at[core], local_sem
+    )
+    ours.start()
+    for i in range(n - 1):
+        back_copy(i, me, me).wait_send()
+    ours.wait()
+    last.wait()
 
 
 def whole_ring(own, enc_mat, dec_mat):
-    n, few, block = own.shape[1:]
-    half = 2 * few
+    n, triple, block = own.shape
+    half = triple // 3 * 2
     depth, share = enc_mat.shape
     vmem = pl.BlockSpec(memory_space=pltpu.VMEM)
     steps = (2, n - 1, PIECES)
@@ -544,7 +590,7 @@
         out_shape=[
             jax.ShapeDtypeStruct((depth, share), BF16),
             jax.ShapeDtypeStruct((depth, share), BF16),
-            jax.ShapeDtypeStruct((n, 3 * few, block), BF16),
+            jax.ShapeDtypeStruct((2, n // 2, triple, block), BF16),
             jax.ShapeDtypeStruct((n, half, 2 * share), BF16),
         ],
         in_specs=[vmem] * 3,
@@ -561,9 +607,12 @@
             pltpu.VMEM((3, n * half + 2 * PAD, LANES), F32),
             pltpu.VMEM(own.shape, BF16),
             pltpu.VMEM(own.shape, BF16),
+            pltpu.VMEM(own.shape, BF16),
+            pltpu.VMEM(own.shape, BF16),
             pltpu.VMEM((depth, share), F32),
             pltpu.VMEM((depth, share), F32),
-            dma(steps), dma(steps), dma(steps), dma(steps), dma, dma((2,)), dma((2,)), dma((2,)),
+            dma(steps), dma(steps), dma(steps), dma(steps), dma, dma((2,)),
+            dma((n,)), dma((n,)), dma((n,)), dma((n,)), dma((n,)), dma((n,)), dma((n,)), dma((n,)), dma, dma,
         ],
         compiler_params=pltpu.CompilerParams(
             collective_id=0, has_side_effects=True, vmem_limit_bytes=56 * 2**20
@@ -584,7 +633,7 @@
     few = half // 2
     block, taps, share = enc_weight.shape
     half_width = cotangent.shape[1]
-    if cores != 2 or taps != 5 or block > LANES or parts * half > 2048:
+    if cores != 2 or taps != 5 or block > LANES or parts * half > 2048 or parts % 2:
         return wide_shards(inputs, enc_weight, dec_weight, cotangent)
     core = lax.axis_index("chan")
 
@@ -593,7 +642,7 @@
     cot_full = lax.all_gather(cotangent, "chan", axis=1, tiled=True)
     cot_some = lax.dynamic_slice_in_dim(cot_full, core * half, half, 0).reshape(few, 2, width)
     leaving = jnp.concatenate([pooled, cot_some[:, 0], cot_some[:, 1]], axis=0)
-    columns = to_columns(leaving, parts).reshape(parts, 3, few, block).transpose(1, 0, 2, 3)
+    columns = leaving.reshape(3 * few, parts, block).transpose(1, 0, 2)
 
     def matrix(weight):
         fill = ((0, 0), (0, LANES - block), (0, 0))
@@ -604,10 +653,8 @@
     def unfold(grad):
         return grad.reshape(taps, LANES, share)[:, :block].transpose(1, 0, 2)
 
-    mine = lax.all_gather(to_rows(back), "chan", axis=0, tiled=False)
     col_start = core * half_width
-    mine = lax.dynamic_slice_in_dim(mine, col_start, half_width, 2).astype(F32)
-    mine = mine.reshape(2, 3, few, half_width)
+    mine = back.astype(F32).transpose(0, 2, 1, 3).reshape(2, 3, few, half_width)
     pool_grad = mine[:, 0].reshape(half, half_width)
     decoded = jnp.stack([mine[:, 1], mine[:, 2]], axis=2).reshape(rows, half_width)
     skip = lax.dynamic_slice_in_dim(inputs, col_start, half_width, 1)

time: 218 us -> 197 us (0.904)
  Pallas kernels: 135 us -> 175 us
  blocking collectives: 23.3 us -> 2.66 us
  waiting for transfers between devices: 19.4 us -> 0 us
  between operations: 14.2 us -> 0.84 us
  starting transfers between devices: 7.55 us -> 0 us
    pallas_call x1, Pallas kernels: 135 us -> 175 us  [whole_ring(): pl.pallas_call(functools.partial(whole_kernel, n), out_shape=[jax.ShapeDt...]
    all_to_all x1 -> x0, blocking collectives: 20.5 us -> none  [to_rows(): got = lax.all_to_all(blocks, 'seq', 0, 0, tiled=True)]
    all_to_all x1 -> x0, waiting for transfers between devices: 13.8 us -> none  [to_columns(): return lax.all_to_all(blocks, 'seq', 0, 0, tiled=True)]
    all_to_all x1 -> x0, starting transfers between devices: 7.33 us -> none  [to_columns(): return lax.all_to_all(blocks, 'seq', 0, 0, tiled=True)]
    all_gather x1 -> x0, waiting for transfers between devices: 5.51 us -> none  [shards(): mine = lax.all_gather(to_rows(back), 'chan', axis=0, tiled=False)]
    transpose x2, local copies, waits for them, and re-layouts: 1.83 us -> 4.13 us  [unfold(): return grad.reshape(taps, LANES, share)[:, :block].transpose(1, 0, 2)]
  transfers between devices with their start and end apart: 2 -> 0, of which waited for: 2 -> 0; matrix products, arithmetic and copies ran while one was open for 2% -> 0% of each run, Pallas kernels for 0% -> 0%
where the time goes in v4:
time: 197 us
  Pallas kernels  175 us (89%)
  local copies, waits for them, and re-layouts  13 us (7%)
  other arithmetic  4.97 us (3%)
  blocking collectives  2.66 us (1%)
    pallas_call x1, Pallas kernels, whole_ring(): pl.pallas_call(functools.partial(whole_kernel, n), out_shape=[jax.ShapeDt...  175 us
    transpose x2, local copies, waits for them, and re-layouts, unfold(): return grad.reshape(taps, LANES, share)[:, :block].transpose(1, 0, 2)  4.13 us

profile of v4, /device:TPU:0, one launch (start us, length us, event | category | flops | bytes accessed | tf_op | source)
XLA Modules:
  0.0 196.8 jit_solution(16284492357680821610)
XLA Ops:
  0.6 2.7 %all_gather.3 = bf16[512,768]{1,0:T(8,128)(2,1)S(1)} all-gather(bf16[512,384]{1,0:T(8,128)(2,1)} %param.7), channel_id=1, replica_groups=mesh['groups'=2,'seq'=8,'chan'=2] {'chan'}, dimensions={1}, use_global_device_ids=true | all-gather | bytes 1179648 | tf_op jit(solution)/shard_map/all_gather | solution.py:642
  3.3 1.1 dynamic-slice_convert_fusion
  4.4 0.5 reshape.64
  4.8 0.9 reduce_sum.9
  5.8 0.2 copy.21
  6.0 0.2 copy.24
  6.2 0.1 reshape.55
  6.3 0.5 fusion
  6.9 0.6 copy.22
  7.5 0.0 copy-start.3
  7.5 0.2 copy.25
  7.7 0.4 copy.23
  8.1 0.2 copy.26
  8.3 1.1 maximum_bitcast_fusion.own_ref
  9.3 1.1 pad.7
  10.4 1.0 pad.8
  11.4 175.4 %shard_map.75 = (bf16[640,768]{1,0:T(8,128)(2,1)}, bf16[640,768]{1,0:T(8,128)(2,1)}, bf16[2,4,384,96]{3,2,1,0:T(8,128)(2,1)}, bf16[8,256,1536]{2,1,0:T(8,128)(2,1)}) custom-call(bf16[8,384,96]{2,1,0:T(8,128)(2,1)} %maximum_bitcast_fusion.own_ref, bf16[640,768]{1,0:T(8,128)(2,1)} %bitcast.25, bf16[640,768]{1,0:T(8,128)(2,1)} %bitcast.26), custom_call_target="tpu_custom_call" | custom-call | flops 12079595520 | bytes 12582912 | tf_op jit(solution)/shard_map/pallas_call | solution.py:588
  186.8 2.1 %slice_bitcast_fusion.1 = bf16[96,5,768]{2,0,1:T(8,128)(2,1)} fusion(bf16[5,128,768]{2,1,0:T(8,128)(2,1)} %bitcast.33), kind=kLoop, calls=%fused_computation.6 | loop fusion | bytes 1474560 | tf_op jit(solution)/shard_map/transpose | solution.py:654
  188.9 2.0 %slice_bitcast_fusion = bf16[96,5,768]{2,0,1:T(8,128)(2,1)} fusion(bf16[5,128,768]{2,1,0:T(8,128)(2,1)} %bitcast.32), kind=kLoop, calls=%fused_computation.5 | loop fusion | bytes 1474560 | tf_op jit(solution)/shard_map/transpose | solution.py:654
  190.9 0.1 convert_bitcast_fusion
  191.1 1.0 copy.27
  192.1 0.8 reshape.66
  192.9 0.1 slice_multiply_fusion
  193.0 0.3 broadcast_in_dim.3
  193.2 0.5 mul.35
  193.8 0.2 copy-done
  193.9 0.8 add_convert_fusion
  194.8 0.1 pad_maximum_fusion
  194.8 0.0 copy-start.1
  194.8 0.6 copy.29
  195.5 0.5 reshape.60
  196.0 0.8 add_convert_fusion.1
  (8 shorter events, 0.0 us)
Async XLA Ops:
  7.5 1.9 copy-start.3
  8.3 2.1 %copy-start.4 = (bf16[96,5,768]{2,0,1:T(8,128)(2,1)S(1)}, bf16[96,5,768]{2,0,1:T(8,128)(2,1)}, u32[]{:S(2)}) copy-start(bf16[96,5,768]{2,0,1:T(8,128)(2,1)} %param.6) | copy-start | bytes 2211844
  186.8 4.1 %copy-start.2 = (bf16[2,4,384,96]{3,2,1,0:T(8,128)(2,1)S(1)}, bf16[2,4,384,96]{3,2,1,0:T(8,128)(2,1)}, u32[]{:S(2)}) copy-start(bf16[2,4,384,96]{3,2,1,0:T(8,128)(2,1)} %get-tuple-element.7) | copy-start | bytes 1769476
  193.0 1.0 copy-start
  194.8 1.2 copy-start.1

commit v5 on v4

--- a/solution.py
+++ b/solution.py
@@ -490,35 +490,44 @@
         for t in range(5):
             add(0, t - 2, g[:, t * LANES : (t + 1) * LANES])
 
-    for d in range(2):
-        consume(me, d, lambda cols: mine[d * side : (d + 1) * side, cols])
-
     def stage_copy(d, s):
         owner = ring_index(signed(d, s + 1), n)
         return pltpu.make_async_copy(
             gathered.at[owner, pl.ds(d * side, side)], stage.at[d], stage_sem.at[d]
         )
 
-    def take(s):
-        for d in range(2):
-            stage_copy(d, s).start()
-        for d in range(2):
-            stage_copy(d, s).wait()
-            consume(ring_index(signed(d, s + 1), n), d, lambda cols: stage[d, :, cols])
+    def take(d, s):
+        stage_copy(d, s).wait()
+        consume(ring_index(signed(d, s + 1), n), d, lambda cols: stage[d, :, cols])
+
+    def pass_on(s, q):
+        for d in range(2):
+            ag_copy(d, s, q, True, s + 1).wait_recv()
+            ag_copy(d, s + 1, q, False, s + 1).start()
+
+    for q in range(PIECES):
+        pass_on(0, q)
+        consume(me, q, lambda cols: mine[q * side : (q + 1) * side, cols])
 
     def ag_step(s, carry):
-        for q in range(PIECES):
-            for d in range(2):
-                ag_copy(d, s, q, True, s + 1).wait_recv()
-                ag_copy(d, s + 1, q, False, s + 1).start()
-        take(s)
-        return carry
-
-    lax.fori_loop(0, n - 2, ag_step, 0)
+        for d in range(2):
+            stage_copy(d, s - 1).start()
+        for q in range(PIECES):
+            pass_on(s, q)
+            take(q, s - 1)
+        return carry
+
+    lax.fori_loop(1, n - 2, ag_step, 0)
+    for d in range(2):
+        stage_copy(d, n - 3).start()
     for q in range(PIECES):
         for d in range(2):
             ag_copy(d, n - 2, q, True, n - 1).wait_recv()
-    take(n - 2)
+        take(q, n - 3)
+    for d in range(2):
+        stage_copy(d, n - 2).start()
+    for d in range(2):
+        take(d, n - 2)
 
     def pick(k, chunk, part):
         at = pl.ds(pl.multiple_of(PAD + chunk * half + part * few, 8), few)
@@ -633,7 +642,7 @@
     few = half // 2
     block, taps, share = enc_weight.shape
     half_width = cotangent.shape[1]
-    if cores != 2 or taps != 5 or block > LANES or parts * half > 2048 or parts % 2:
+    if cores != 2 or taps != 5 or block > LANES or parts * half > 2048 or parts % 2 or parts < 4:
         return wide_shards(inputs, enc_weight, dec_weight, cotangent)
     core = lax.axis_index("chan")
 

time: 197 us -> 198 us (level)
  no operation moved by 1% of the time
where the time goes in v5:
time: 198 us
  Pallas kernels  176 us (89%)
  local copies, waits for them, and re-layouts  12.8 us (6%)
  other arithmetic  4.97 us (3%)
  blocking collectives  2.66 us (1%)
    pallas_call x1, Pallas kernels, whole_ring(): pl.pallas_call(functools.partial(whole_kernel, n), out_shape=[jax.ShapeDt...  176 us
    transpose x2, local copies, waits for them, and re-layouts, unfold(): return grad.reshape(taps, LANES, share)[:, :block].transpose(1, 0, 2)  4.13 us

profile of v5, /device:TPU:0, one launch (start us, length us, event | category | flops | bytes accessed | tf_op | source)
XLA Modules:
  0.0 197.8 jit_solution(2482734173093646590)
XLA Ops:
  0.6 2.7 %all_gather.3 = bf16[512,768]{1,0:T(8,128)(2,1)S(1)} all-gather(bf16[512,384]{1,0:T(8,128)(2,1)} %param.7), channel_id=1, replica_groups=mesh['groups'=2,'seq'=8,'chan'=2] {'chan'}, dimensions={1}, use_global_device_ids=true | all-gather | bytes 1179648 | tf_op jit(solution)/shard_map/all_gather | solution.py:651
  3.3 1.1 dynamic-slice_convert_fusion
  4.4 0.5 reshape.64
  4.8 0.9 reduce_sum.9
  5.8 0.2 copy.21
  6.0 0.2 copy.24
  6.2 0.1 reshape.55
  6.3 0.5 fusion
  6.9 0.4 copy.22
  7.3 0.0 copy-start.3
  7.3 0.2 copy.25
  7.5 0.4 copy.23
  7.9 0.2 copy.26
  8.1 0.0 copy-start.4
  8.1 1.1 maximum_bitcast_fusion.own_ref
  9.2 1.1 pad.7
  10.2 1.0 pad.8
  11.2 176.5 %shard_map.75 = (bf16[640,768]{1,0:T(8,128)(2,1)}, bf16[640,768]{1,0:T(8,128)(2,1)}, bf16[2,4,384,96]{3,2,1,0:T(8,128)(2,1)}, bf16[8,256,1536]{2,1,0:T(8,128)(2,1)}) custom-call(bf16[8,384,96]{2,1,0:T(8,128)(2,1)} %maximum_bitcast_fusion.own_ref, bf16[640,768]{1,0:T(8,128)(2,1)} %bitcast.25, bf16[640,768]{1,0:T(8,128)(2,1)} %bitcast.26), custom_call_target="tpu_custom_call" | custom-call | flops 12079595520 | bytes 12582912 | tf_op jit(solution)/shard_map/pallas_call | solution.py:597
  187.7 2.1 %slice_bitcast_fusion.1 = bf16[96,5,768]{2,0,1:T(8,128)(2,1)} fusion(bf16[5,128,768]{2,1,0:T(8,128)(2,1)} %bitcast.33), kind=kLoop, calls=%fused_computation.6 | loop fusion | bytes 1474560 | tf_op jit(solution)/shard_map/transpose | solution.py:663
  189.8 2.0 %slice_bitcast_fusion = bf16[96,5,768]{2,0,1:T(8,128)(2,1)} fusion(bf16[5,128,768]{2,1,0:T(8,128)(2,1)} %bitcast.32), kind=kLoop, calls=%fused_computation.5 | loop fusion | bytes 1474560 | tf_op jit(solution)/shard_map/transpose | solution.py:663
  191.9 0.1 convert_bitcast_fusion
  192.0 1.0 copy.27
  193.0 0.8 reshape.66
  193.8 0.1 slice_multiply_fusion
  193.9 0.3 broadcast_in_dim.3
  194.2 0.5 mul.35
  194.7 0.2 copy-done
  194.9 0.8 add_convert_fusion
  195.7 0.1 pad_maximum_fusion
  195.7 0.6 copy.29
  196.4 0.5 reshape.60
  196.9 0.8 add_convert_fusion.1
  (8 shorter events, 0.0 us)
Async XLA Ops:
  7.3 1.9 copy-start.3
  8.1 2.1 %copy-start.4 = (bf16[96,5,768]{2,0,1:T(8,128)(2,1)S(1)}, bf16[96,5,768]{2,0,1:T(8,128)(2,1)}, u32[]{:S(2)}) copy-start(bf16[96,5,768]{2,0,1:T(8,128)(2,1)} %param.6) | copy-start | bytes 2211844
  187.7 4.1 %copy-start.2 = (bf16[2,4,384,96]{3,2,1,0:T(8,128)(2,1)S(1)}, bf16[2,4,384,96]{3,2,1,0:T(8,128)(2,1)}, u32[]{:S(2)}) copy-start(bf16[2,4,384,96]{3,2,1,0:T(8,128)(2,1)} %get-tuple-element.7) | copy-start | bytes 1769476
  193.9 1.0 copy-start
  195.7 1.2 copy-start.1
